TPU v7x, 256 devices: a whole 4x4x8 slice. The times are simulated.
256 devices in a mesh: rec: 32 (over x, z), head: 8 (over y, core).
Axes of the slice: x: 4, y: 4, z: 8, core: 2. Of those that a mesh axis runs over, the one named last changes fastest.
Arguments:
- spectrogram: bfloat16 [32, 1536, 8192], P('rec', 'head'), may hold values from -8 to 8
- epoch_counts: int32 [32], P('rec'), may hold values from 1 to 1536, as said below
- conv_first: bfloat16 [7, 64, 256], replicated, may hold values from -0.25 to 0.25
- bias_first: float32 [256], replicated, may hold values from -3 to 3
- conv_second: bfloat16 [7, 256, 1024], replicated, may hold values from -0.125 to 0.125
- bias_second: float32 [1024], replicated, may hold values from -3 to 3
- projection: bfloat16 [1024, 3, 1024], replicated
Outputs:
- attended: bfloat16 [32, 1536, 1024], P('rec', None, 'head')
Inputs may be any that keep to these rules, and one draw needn't show every extreme that they name: Recording r has valid epochs in slots 0 to epoch_counts[r] - 1; some recording fills all 1536 slots.
All inputs are finite; a program needn't handle non-finite values.
Results may differ from a plain program's by a relative error of at most 0.018.
Values may be sent and summed in bfloat16 or wider, within the bound.
A program may use at most 64 MiB of HBM per device.

v0:
```python
import jax
import jax.numpy as jnp
from jax import lax
from jax.sharding import PartitionSpec as P

HD = 64
TILE = 16


def conv_layer(inputs, weight, biases):
    number, length, channels = inputs.shape
    kernel_len = weight.shape[0]
    padded = jnp.pad(inputs, ((0, 0), (kernel_len // 2, kernel_len // 2), (0, 0)))
    columns = jnp.stack(
        [padded[:, offset : offset + length : 2, :] for offset in range(kernel_len)], axis=2
    )
    columns = columns.reshape(number * (length // 2), kernel_len * channels)
    result = (
        jnp.dot(
            columns,
            weight.reshape(kernel_len * channels, weight.shape[2]),
            preferred_element_type=jnp.float32,
        )
        + biases
    )
    return result.reshape(number, length // 2, weight.shape[2])


def embed_block(tile_rows, conv_first, bias_first, conv_second, bias_second):
    epochs_here = tile_rows.shape[0]
    channels = conv_first.shape[1]
    spectra = tile_rows.reshape(epochs_here, tile_rows.shape[1] // channels, channels)
    hidden = jax.nn.gelu(conv_layer(spectra, conv_first, bias_first)).astype(jnp.bfloat16)
    deeper = jax.nn.gelu(conv_layer(hidden, conv_second, bias_second))
    return jnp.mean(deeper, axis=1).astype(jnp.bfloat16)


def embed_live(epoch_rows, live_flags, conv_first, bias_first, conv_second, bias_second):
    row_total = epoch_rows.shape[0]
    out_width = conv_second.shape[2]
    is_live = live_flags > 0
    sort_order = jnp.argsort(jnp.where(is_live, 0, 1).astype(jnp.int32), stable=True)
    live_count = jnp.sum(is_live.astype(jnp.int32))
    padded_total = -(-row_total // TILE) * TILE
    packed = epoch_rows[sort_order]

    def one_tile(tile_index, buffer):
        first_row = tile_index * TILE
        tile_rows = lax.dynamic_slice_in_dim(packed, first_row, TILE, 0)
        embedded = embed_block(tile_rows, conv_first, bias_first, conv_second, bias_second)
        inside = first_row + jnp.arange(TILE, dtype=jnp.int32) < live_count
        embedded = jnp.where(inside[:, None], embedded, jnp.zeros_like(embedded))
        return lax.dynamic_update_slice_in_dim(buffer, embedded, first_row, 0)

    tile_count = (live_count + TILE - 1) // TILE
    buffer = lax.fori_loop(
        0, tile_count, one_tile, jnp.zeros((padded_total, out_width), jnp.bfloat16)
    )
    return jnp.zeros((row_total, out_width), jnp.bfloat16).at[sort_order].set(buffer)


def shards(spectrogram, epoch_counts, conv_first, bias_first, conv_second, bias_second, projection):
    slot_count = spectrogram.shape[1]
    row_width = spectrogram.shape[2]
    epoch_rows = spectrogram[0]
    head_index = lax.axis_index("head")
    recorded = epoch_counts[0]
    global_slot = head_index * slot_count + jnp.arange(slot_count, dtype=jnp.int32)
    live_flags = (global_slot < recorded).astype(jnp.bfloat16)
    devices_rec = lax.axis_size("rec")
    heads_dev = lax.axis_size("head")
    groups = slot_count // devices_rec
    spread_rows = epoch_rows.reshape(groups, devices_rec, row_width)
    spread_flags = live_flags.reshape(groups, devices_rec)
    rows_part = lax.all_to_all(spread_rows, "rec", split_axis=1, concat_axis=1, tiled=True)
    flags_part = lax.all_to_all(spread_flags, "rec", split_axis=1, concat_axis=1, tiled=True)
    groups = rows_part.shape[0]
    embed_rows_part = rows_part.reshape(groups * devices_rec, rows_part.shape[2])
    embed_flags_part = flags_part.reshape(groups * devices_rec)
    embedded = embed_live(
        embed_rows_part, embed_flags_part, conv_first, bias_first, conv_second, bias_second
    )
    embedded = embedded.reshape(groups, devices_rec, embedded.shape[1])
    remote = lax.all_to_all(embedded, "rec", split_axis=1, concat_axis=1, tiled=True)
    embedded = remote.reshape(slot_count, remote.shape[2])
    model_width = projection.shape[0]
    group_width = model_width // heads_dev
    mixed_rows = jnp.dot(
        embedded,
        projection.reshape(model_width, 3 * model_width),
        preferred_element_type=jnp.float32,
    ).astype(jnp.bfloat16)
    mixed_rows = mixed_rows.reshape(slot_count, 3, heads_dev, group_width)
    regrouped = lax.all_to_all(mixed_rows, "head", split_axis=2, concat_axis=0, tiled=True)
    regrouped = regrouped.reshape(slot_count * heads_dev, 3, group_width)
    epoch_total = regrouped.shape[0]
    heads_here = group_width // HD
    queries = regrouped[:, 0].reshape(epoch_total, heads_here, HD)
    key_rows = regrouped[:, 1].reshape(epoch_total, heads_here, HD)
    values = regrouped[:, 2].reshape(epoch_total, heads_here, HD)
    key_live = jnp.arange(epoch_total, dtype=jnp.int32) < recorded
    scores = jnp.einsum(
        "qhd,khd->hqk", queries, key_rows, preferred_element_type=jnp.float32
    ) * HD ** (-0.5)
    scores = jnp.where(key_live[None, None, :], scores, -1e30)
    row_max = jnp.max(scores, axis=-1, keepdims=True)
    powered = jnp.exp(scores - row_max)
    probabilities = (powered / jnp.sum(powered, axis=-1, keepdims=True)).astype(jnp.bfloat16)
    attended = jnp.einsum("hqk,khd->qhd", probabilities, values, preferred_element_type=jnp.float32)
    attended = jnp.where(key_live[:, None, None], attended, jnp.zeros_like(attended))
    return attended.reshape(1, epoch_total, group_width).astype(jnp.bfloat16)


def solution(mesh):
    return jax.shard_map(
        shards,
        mesh=mesh,
        in_specs=(P("rec", "head", None), P("rec"), P(), P(), P(), P(), P()),
        out_specs=P("rec", None, "head"),
        check_vma=False,
    )
```

profile of v0, /device:TPU:1, one launch (start us, length us, event | category | flops | bytes accessed | tf_op | source)
XLA Modules:
  0.0 488.8 jit_solution(16371102799083188510)
XLA Ops:
  1.4 11.9 %all-to-all-start = ((bf16[6,32,1]{0,2,1:T(2,128)(2,1)}), bf16[6,32,1]{0,2,1:T(2,128)(2,1)S(1)}, u32[]{:S(2)}, u32[]{:S(2)}) async-start(bf16[6,32,1]{0,2,1:T(2,128)(2,1)} %copy.62), calls=%async_computation | async-start | bytes 32768 | tf_op jit(solution)/shard_map/all_to_all | solution.py:76
  13.3 5.6 %copy.64 = bf16[6,32,8192]{2,0,1:T(8,128)(2,1)} copy(bf16[6,32,8192]{2,1,0:T(8,128)(2,1)} %bitcast.131) | data formatting | bytes 6291456 | tf_op jit(solution)/shard_map/reshape;squeeze | solution.py:73
  21.8 6.4 %all-to-all-start.1 = ((bf16[6,32,8192]{2,0,1:T(8,128)(2,1)}), bf16[6,32,8192]{2,0,1:T(8,128)(2,1)}, u32[]{:S(2)}, u32[]{:S(2)}) async-start(bf16[6,32,8192]{2,0,1:T(8,128)(2,1)} %copy.64), calls=%async_computation.1 | async-start | bytes 8388608 | tf_op jit(solution)/shard_map/all_to_all | solution.py:75
  32.9 89.3 %all-to-all-done.1 = bf16[6,32,8192]{2,0,1:T(8,128)(2,1)} async-done(((bf16[6,32,8192]{2,0,1:T(8,128)(2,1)}), bf16[6,32,8192]{2,0,1:T(8,128)(2,1)}, u32[]{:S(2)}, u32[]{:S(2)}) %all-to-all-start.1) | async-done | bytes 3145760 | tf_op jit(solution)/shard_map/all_to_all | solution.py:75
  122.2 3.9 copy.65
  126.1 4.2 gather_fusion
  130.4 242.4 %while.12 = (s32[]{:T(128)}, bf16[192,1024]{1,0:T(8,128)(2,1)S(1)}, s32[]{:T(128)}, s32[]{:T(128)}, bf16[192,8192]{1,0:T(8,128)(2,1)}, /*index=5*/bf16[7,64,256]...) while((s32[]{:T(128)}, bf16[192,1024]{1,0:T(8,128)(2,1)S(1)}, ...), condition=%wide.region_4.5_spmd, body=%wide.region_2.4_spmd.sunk | while | flops 2121826304 | bytes 49743604 | solution.py:56
  139.5 3.5 copy.82
  163.7 3.5 copy.82
  187.9 3.5 copy.82
  212.1 3.5 copy.82
  236.4 3.5 copy.82
  260.6 3.5 copy.82
  284.8 3.5 copy.82
  309.0 3.5 copy.82
  333.2 3.5 copy.82
  357.5 3.5 copy.82
  375.4 8.5 %all-to-all-start.2 = ((bf16[6,32,1024]{2,0,1:T(8,128)(2,1)}), bf16[6,32,1024]{2,0,1:T(8,128)(2,1)S(1)}, u32[]{:S(2)}, u32[]{:S(2)}) async-start(bf16[6,32,1024]{2,0,1:T(8,128)(2,1)} %copy.66), calls=%async_computation.2 | async-start | bytes 1048576 | tf_op jit(solution)/shard_map/all_to_all | solution.py:84
  383.9 8.7 %copy.68 = bf16[1024,3,1024]{0,2,1:T(8,128)(2,1)} copy(bf16[1024,3,1024]{2,0,1:T(8,128)(2,1)} %param.15) | data formatting | bytes 12582912 | tf_op args[6]
  395.3 5.0 %fusion.28 = bf16[24,8,24,128]{3,1,2,0:T(8,128)(2,1)S(1)} fusion(bf16[192,1024]{1,0:T(8,128)(2,1)S(1)} %bitcast.133, bf16[1024,3072]{0,1:T(8,128)(2,1)} %bitcast.128), kind=kOutput, calls=%fused_computation.54 | convolution fusion | flops 1208549376 | bytes 7864320 | tf_op jit(solution)/shard_map/dot_general | solution.py:88
  401.7 53.8 %all-to-all-start.3 = ((bf16[192,3,8,128]{3,0,1,2:T(8,128)(2,1)}), bf16[192,3,8,128]{3,0,1,2:T(8,128)(2,1)S(1)}, u32[]{:S(2)}, u32[]{:S(2)}) async-start(bf16[192,3,8,128]{3,0,1,2:T(8,128)(2,1)} %copy.69), calls=%async_computation.3 | async-start | bytes 2359296 | tf_op jit(solution)/shard_map/all_to_all | solution.py:94
  455.6 16.5 %all-to-all-done.3 = bf16[192,3,8,128]{3,0,1,2:T(8,128)(2,1)S(1)} async-done(((bf16[192,3,8,128]{3,0,1,2:T(8,128)(2,1)}), bf16[192,3,8,128]{3,0,1,2:T(8,128)(2,1)S(1)}, u32[]{:S(2)}, u32[]{:S(2)}) %all-to-all-start.3) | async-done | bytes 1179680 | tf_op jit(solution)/shard_map/all_to_all | solution.py:94
  472.8 6.9 %fusion.40 = f32[2,1536]{1,0:T(2,128)S(1)} fusion(pred[1536]{0:T(1024)(128)(4,1)S(1)} %iota_compare_fusion, bf16[1536,2,64]{0,2,1:T(8,128)(2,1)S(1)} %bitcast.134, bf16[1536,2,64]{0,2,1:T(8,128)(2,1)S(1)} %bitcast.136), kind=kOutput, calls=%fused_computation.70 | convolution fusion | flops 622855680 | bytes 800256 | tf_op jit(solution)/shard_map/sub | solution.py:107
  479.7 8.2 %fusion.27 = bf16[2,64,1536]{2,1,0:T(8,128)(2,1)S(1)} fusion(bf16[1536,2,64]{0,2,1:T(8,128)(2,1)S(1)} %bitcast.138, f32[2,1536]{1,0:T(2,128)S(1)} %fusion.40, pred[1536]{0:T(1024)(128)(4,1)S(1)} %iota_compare_fusion, bf16[1536,2,64]{0,2,1:T(8,128)(2,1)S(1)} %bitcast.135, bf16[1536,2,64]{0,2,1:T(8,128)(2,1)S(1)} %bitcast.137), kind=kOutput, calls=%fused_computation.53 | convolution fusion | flops 1231950336 | bytes 1586688 | tf_op jit(solution)/shard_map/hqk,khd->qhd/dot_general | solution.py:109
  (450 shorter events, 221.1 us)
Async XLA Ops:
  1.4 20.4 %all-to-all-start = ((bf16[6,32,1]{0,2,1:T(2,128)(2,1)}), bf16[6,32,1]{0,2,1:T(2,128)(2,1)S(1)}, u32[]{:S(2)}, u32[]{:S(2)}) async-start(bf16[6,32,1]{0,2,1:T(2,128)(2,1)} %copy.62), calls=%async_computation | async-start | bytes 32768 | tf_op jit(solution)/shard_map/all_to_all | solution.py:76
  21.8 100.3 %all-to-all-start.1 = ((bf16[6,32,8192]{2,0,1:T(8,128)(2,1)}), bf16[6,32,8192]{2,0,1:T(8,128)(2,1)}, u32[]{:S(2)}, u32[]{:S(2)}) async-start(bf16[6,32,8192]{2,0,1:T(8,128)(2,1)} %copy.64), calls=%async_computation.1 | async-start | bytes 8388608 | tf_op jit(solution)/shard_map/all_to_all | solution.py:75
  126.1 4.3 copy-start.1
  126.1 4.3 copy-start.2
  126.1 4.3 copy-start.3
  149.4 2.0 copy-start
  173.6 2.0 copy-start
  197.9 2.0 copy-start
  222.1 2.0 copy-start
  246.3 2.0 copy-start
  270.5 2.0 copy-start
  294.8 2.0 copy-start
  319.0 2.0 copy-start
  343.2 2.0 copy-start
  367.4 2.0 copy-start
  375.4 19.6 %all-to-all-start.2 = ((bf16[6,32,1024]{2,0,1:T(8,128)(2,1)}), bf16[6,32,1024]{2,0,1:T(8,128)(2,1)S(1)}, u32[]{:S(2)}, u32[]{:S(2)}) async-start(bf16[6,32,1024]{2,0,1:T(8,128)(2,1)} %copy.66), calls=%async_computation.2 | async-start | bytes 1048576 | tf_op jit(solution)/shard_map/all_to_all | solution.py:84
  401.7 70.4 %all-to-all-start.3 = ((bf16[192,3,8,128]{3,0,1,2:T(8,128)(2,1)}), bf16[192,3,8,128]{3,0,1,2:T(8,128)(2,1)S(1)}, u32[]{:S(2)}, u32[]{:S(2)}) async-start(bf16[192,3,8,128]{3,0,1,2:T(8,128)(2,1)} %copy.69), calls=%async_computation.3 | async-start | bytes 2359296 | tf_op jit(solution)/shard_map/all_to_all | solution.py:94
where the time goes:
time: 491 us; the launch traced here: 489 us
  local copies, waits for them, and re-layouts  227 us (46%)
  waiting for transfers between devices  111 us (23%)
  starting transfers between devices  80.6 us (16%)
  matrix products  51.6 us (11%)
  other arithmetic  14.3 us (3%)
    all_to_all x1, waiting for transfers between devices, shards(): lax.all_to_all(spread_rows, 'rec', split_axis=1, concat_axis=1, tiled=True)  89.3 us
    while x150, local copies, waits for them, and re-layouts  64.8 us
    another operation x40, local copies, waits for them, and re-layouts, conv_layer(): jnp.stack([padded[:, offset:offset + length:2, :] for offset in range(ker...  55 us
    all_to_all x1, starting transfers between devices, shards(): lax.all_to_all(mixed_rows, 'head', split_axis=2, concat_axis=0, tiled=True)  53.8 us
    slice x140, local copies, waits for them, and re-layouts, conv_layer(): padded[:, offset:offset + length:2, :]  45.9 us
    dot_general x20, matrix products, conv_layer(): jnp.dot(columns, weight.reshape(kernel_len * channels, weight.shape[2]),...  31.5 us
    all_to_all x1, waiting for transfers between devices, shards(): lax.all_to_all(mixed_rows, 'head', split_axis=2, concat_axis=0, tiled=True)  16.5 us
    reshape x10, local copies, waits for them, and re-layouts, conv_layer(): columns = columns.reshape(number * (length // 2), kernel_len * channels)  13.1 us
  transfers between devices with their start and end apart: 4, of which 4 were waited for; matrix products, arithmetic and copies ran while one was open for 4% of the time, Pallas kernels for 0%

commit v1 on v0

v1 whole, which is shorter than its diff:
```python
import functools

import jax
import jax.numpy as jnp
from jax import lax
from jax.experimental import pallas as pl
from jax.experimental.pallas import tpu as pltpu
from jax.sharding import PartitionSpec as P

HD = 64
ROOT = 0.7978845608028654
CUBE = ROOT * 0.044715
GROUP = 4


def gelu_twice(y):
    return y + y * jnp.tanh(y * (ROOT + CUBE * (y * y)))


def embed_kernel(x_ref, w1_ref, b1_ref, w2_ref, b2_ref, o_ref, h_ref, acc_ref, w1p_ref):
    rows = x_ref.shape[0]
    taps, c0, c1 = w1_ref.shape
    wide = (taps + 1) * c0
    frames = x_ref.shape[1] // (2 * c0)
    lane = 2 * c0
    w1p_ref[0:c0, :] = jnp.zeros((c0, c1), jnp.bfloat16)
    w1p_ref[c0:wide, :] = w1_ref[...].reshape(taps * c0, c1)
    blank = jnp.zeros((rows, c1), jnp.bfloat16)
    for t in (0, 1, 2, frames + 3, frames + 4, frames + 5):
        h_ref[t] = blank
    bias = b1_ref[...]

    def first(t, lhs, weight):
        y = jnp.dot(lhs, weight, preferred_element_type=jnp.float32) + bias
        h_ref[t + 3] = (0.5 * gelu_twice(y)).astype(jnp.bfloat16)

    first(0, x_ref[:, 0 : 2 * lane], w1p_ref[2 * lane : 4 * lane, :])
    first(1, x_ref[:, 0 : 3 * lane], w1p_ref[lane : 4 * lane, :])
    first(frames - 1, x_ref[:, (frames - 3) * lane : frames * lane], w1p_ref[0 : 3 * lane, :])

    def first_step(i, _):
        start = pl.multiple_of(i * lane, lane)
        first(i + 2, x_ref[:, pl.ds(start, wide)], w1p_ref[...])
        return 0

    lax.fori_loop(0, frames - 3, first_step, 0)
    acc_ref[...] = jnp.zeros_like(acc_ref)
    half = frames // 2

    def second_step(i, _):
        for n in range(acc_ref.shape[1] // c1):
            cols = slice(n * c1, (n + 1) * c1)
            lhs = jnp.concatenate(
                [
                    jnp.concatenate([h_ref[2 * (i * GROUP + g) + k] for k in range(taps)], axis=1)
                    for g in range(GROUP)
                ],
                axis=0,
            )
            y = jnp.dot(lhs, w2_ref[:, cols], preferred_element_type=jnp.float32) + b2_ref[:, cols]
            y = gelu_twice(y)
            total = y[0:rows]
            for g in range(1, GROUP):
                total = total + y[g * rows : (g + 1) * rows]
            acc_ref[:, cols] += total
        return 0

    lax.fori_loop(0, half // GROUP, second_step, 0)
    o_ref[...] = (acc_ref[...] * (0.5 / half)).astype(jnp.bfloat16)


def embed(x, w1, b1, w2, b2):
    rows = x.shape[0]
    taps, c0, c1 = w1.shape
    width = w2.shape[2]
    frames = x.shape[1] // (2 * c0)
    return pl.pallas_call(
        embed_kernel,
        out_shape=jax.ShapeDtypeStruct((rows, width), jnp.bfloat16),
        scratch_shapes=[
            pltpu.VMEM((frames + 6, rows, c1), jnp.bfloat16),
            pltpu.VMEM((rows, width), jnp.float32),
            pltpu.VMEM(((taps + 1) * c0, c1), jnp.bfloat16),
        ],
        compiler_params=pltpu.CompilerParams(vmem_limit_bytes=48 * 1024 * 1024),
        name="embed",
    )(x, w1, b1.reshape(1, -1), w2.reshape(taps * c1, width), b2.reshape(1, -1))


def shards(spectrogram, epoch_counts, conv_first, bias_first, conv_second, bias_second, projection):
    recorded = epoch_counts[0]
    embedded = embed(spectrogram[0], conv_first, bias_first, conv_second, bias_second)
    slot_count = embedded.shape[0]
    heads_dev = lax.axis_size("head")
    model_width = projection.shape[0]
    group_width = model_width // heads_dev
    mixed_rows = jnp.dot(
        embedded,
        projection.reshape(model_width, 3 * model_width),
        preferred_element_type=jnp.float32,
    ).astype(jnp.bfloat16)
    mixed_rows = mixed_rows.reshape(slot_count, 3, heads_dev, group_width)
    regrouped = lax.all_to_all(mixed_rows, "head", split_axis=2, concat_axis=0, tiled=True)
    regrouped = regrouped.reshape(slot_count * heads_dev, 3, group_width)
    epoch_total = regrouped.shape[0]
    heads_here = group_width // HD
    queries = regrouped[:, 0].reshape(epoch_total, heads_here, HD)
    key_rows = regrouped[:, 1].reshape(epoch_total, heads_here, HD)
    values = regrouped[:, 2].reshape(epoch_total, heads_here, HD)
    key_live = jnp.arange(epoch_total, dtype=jnp.int32) < recorded
    scores = jnp.einsum(
        "qhd,khd->hqk", queries, key_rows, preferred_element_type=jnp.float32
    ) * HD ** (-0.5)
    scores = jnp.where(key_live[None, None, :], scores, -1e30)
    row_max = jnp.max(scores, axis=-1, keepdims=True)
    powered = jnp.exp(scores - row_max)
    probabilities = (powered / jnp.sum(powered, axis=-1, keepdims=True)).astype(jnp.bfloat16)
    attended = jnp.einsum("hqk,khd->qhd", probabilities, values, preferred_element_type=jnp.float32)
    attended = jnp.where(key_live[:, None, None], attended, jnp.zeros_like(attended))
    return attended.reshape(1, epoch_total, group_width).astype(jnp.bfloat16)


def solution(mesh):
    return jax.shard_map(
        shards,
        mesh=mesh,
        in_specs=(P("rec", "head", None), P("rec"), P(), P(), P(), P(), P()),
        out_specs=P("rec", None, "head"),
        check_vma=False,
    )
```

time: 491 us -> 98.5 us (0.20)
  local copies, waits for them, and re-layouts: 227 us -> 11.9 us
  waiting for transfers between devices: 111 us -> 15.9 us
  starting transfers between devices: 80.6 us -> 6.69 us
  Pallas kernels: 0 us -> 45.8 us
  matrix products: 51.6 us -> 17.2 us
  other arithmetic: 14.3 us -> 0.01 us
    all_to_all x3 -> x0, waiting for transfers between devices: 94.7 us -> none  [the longest x1 89.3 us: shards(): lax.all_to_all(spread_rows, 'rec', split_axis=1, concat_axis=1, tiled=True)]
    while x150 -> x0, local copies, waits for them, and re-layouts: 64.8 us -> none
    another operation x42 -> x0, local copies, waits for them, and re-layouts: 60.7 us -> none  [the longest x40 55 us: conv_layer(): jnp.stack([padded[:, offset:offset + length:2, :] for offset in range(ker...]
    all_to_all x1, starting transfers between devices: 53.8 us -> 6.69 us  [shards(): lax.all_to_all(mixed_rows, 'head', split_axis=2, concat_axis=0, tiled=True)]
    slice x140 -> x0, local copies, waits for them, and re-layouts: 45.9 us -> none  [conv_layer(): padded[:, offset:offset + length:2, :]]
    pallas_call x0 -> x1, Pallas kernels: none -> 45.8 us  [embed(): pl.pallas_call(embed_kernel, out_shape=jax.ShapeDtypeStruct((rows, width)...]
    dot_general x20 -> x0, matrix products: 31.5 us -> none  [conv_layer(): jnp.dot(columns, weight.reshape(kernel_len * channels, weight.shape[2]),...]
    all_to_all x3 -> x0, starting transfers between devices: 26.8 us -> none  [the longest x1 11.9 us: shards(): lax.all_to_all(spread_flags, 'rec', split_axis=1, concat_axis=1, tiled=True)]
  transfers between devices with their start and end apart: 4 -> 1, of which waited for: 4 -> 1; matrix products, arithmetic and copies ran while one was open for 4% -> 0% of each run, Pallas kernels for 0% -> 0%
where the time goes in v1:
time: 98.5 us; the launch traced here: 98.2 us
  Pallas kernels  45.8 us (46%)
  matrix products  17.2 us (17%)
  waiting for transfers between devices  15.9 us (16%)
  local copies, waits for them, and re-layouts  11.9 us (12%)
  starting transfers between devices  6.69 us (7%)
    pallas_call x1, Pallas kernels, embed(): pl.pallas_call(embed_kernel, out_shape=jax.ShapeDtypeStruct((rows, width)...  45.8 us
    all_to_all x1, waiting for transfers between devices, shards(): lax.all_to_all(mixed_rows, 'head', split_axis=2, concat_axis=0, tiled=True)  15.9 us
    unnamed x12, local copies, waits for them, and re-layouts  9.02 us
    dot_general x1, matrix products, shards(): jnp.einsum('hqk,khd->qhd', probabilities, values, preferred_element_type=...  8.19 us
    sub x1, matrix products, shards(): powered = jnp.exp(scores - row_max)  6.77 us
    all_to_all x1, starting transfers between devices, shards(): lax.all_to_all(mixed_rows, 'head', split_axis=2, concat_axis=0, tiled=True)  6.69 us
    dot_general x1, matrix products, shards(): jnp.dot(embedded, projection.reshape(model_width, 3 * model_width), prefe...  2.21 us
  transfers between devices with their start and end apart: 1, of which 1 were waited for; matrix products, arithmetic and copies ran while one was open for 0% of the time, Pallas kernels for 0%

profile of v1, /device:TPU:1, one launch (start us, length us, event | category | flops | bytes accessed | tf_op | source)
XLA Modules:
  0.0 98.2 jit_solution(16416552920192056272)
XLA Ops:
  0.0 0.0 copy-start
  0.0 0.0 copy-start.3
  0.0 0.0 copy-start.2
  0.0 0.0 copy-start.1
  0.0 8.8 %copy.17 = bf16[1024,3,1024]{0,2,1:T(8,128)(2,1)} copy(bf16[1024,3,1024]{2,0,1:T(8,128)(2,1)} %param.13) | data formatting | bytes 12582912 | tf_op args[6]
  8.8 0.0 copy-done
  8.8 0.0 copy-done.3
  8.8 0.0 copy-done.2
  8.8 0.0 copy-done.1
  8.9 45.8 %embed.1 = bf16[192,1024]{1,0:T(8,128)(2,1)S(1)} custom-call(bf16[192,8192]{1,0:T(8,128)(2,1)S(1)} %bitcast.29, bf16[7,64,256]{2,1,0:T(8,128)(2,1)S(1)} %copy-done.1, f32[1,256]{1,0:T(1,128)S(1)} %bitcast.31, bf16[1792,1024]{1,0:T(8,128)(2,1)} %bitcast.35, f32[1,1024]{1,0:T(1,128)S(1)} %bitcast.30), custom_call_target="tpu_custom_call" | custom-call | tf_op jit(solution)/shard_map/embed/pallas_call | solution.py:77
  54.7 0.0 copy-done.4
  54.7 2.2 %fusion.10 = bf16[24,8,24,128]{3,1,2,0:T(8,128)(2,1)S(1)} fusion(bf16[192,1024]{1,0:T(8,128)(2,1)S(1)} %embed.1, bf16[1024,3072]{0,1:T(8,128)(2,1)S(1)} %bitcast.32), kind=kOutput, calls=%fused_computation.13 | convolution fusion | flops 1208549376 | bytes 7864320 | tf_op jit(solution)/shard_map/dot_general | solution.py:97
  56.9 0.2 copy.26
  57.1 1.3 %copy.18 = bf16[192,3,8,128]{3,0,1,2:T(8,128)(2,1)} copy(bf16[192,3,8,128]{3,2,1,0:T(8,128)(2,1)S(1)} %bitcast.34) | data formatting | bytes 2359296 | tf_op jit(solution)/shard_map/reshape | solution.py:102
  58.4 6.7 %all-to-all-start = ((bf16[192,3,8,128]{3,0,1,2:T(8,128)(2,1)}), bf16[192,3,8,128]{3,0,1,2:T(8,128)(2,1)S(1)}, u32[]{:S(2)}, u32[]{:S(2)}) async-start(bf16[192,3,8,128]{3,0,1,2:T(8,128)(2,1)} %copy.18), calls=%async_computation | async-start | bytes 2359296 | tf_op jit(solution)/shard_map/all_to_all | solution.py:103
  65.8 15.9 %all-to-all-done = bf16[192,3,8,128]{3,0,1,2:T(8,128)(2,1)S(1)} async-done(((bf16[192,3,8,128]{3,0,1,2:T(8,128)(2,1)}), bf16[192,3,8,128]{3,0,1,2:T(8,128)(2,1)S(1)}, u32[]{:S(2)}, u32[]{:S(2)}) %all-to-all-start) | async-done | bytes 1179680 | tf_op jit(solution)/shard_map/all_to_all | solution.py:103
  81.6 0.1 copy.19
  81.7 0.1 fusion.18
  81.8 0.2 copy.21
  82.0 0.2 copy.22
  82.2 0.2 copy.20
  82.3 6.8 %fusion.19 = f32[2,1536]{1,0:T(2,128)S(1)} fusion(pred[1536]{0:T(1024)(128)(4,1)S(1)} %iota_compare_fusion, bf16[1536,2,64]{0,2,1:T(8,128)(2,1)S(1)} %bitcast.36, bf16[1536,2,64]{0,2,1:T(8,128)(2,1)S(1)} %bitcast.38), kind=kOutput, calls=%fused_computation.21 | convolution fusion | flops 622855680 | bytes 800256 | tf_op jit(solution)/shard_map/sub | solution.py:116
  89.1 8.2 %fusion.9 = bf16[2,64,1536]{2,1,0:T(8,128)(2,1)S(1)} fusion(bf16[1536,2,64]{0,2,1:T(8,128)(2,1)S(1)} %bitcast.40, f32[2,1536]{1,0:T(2,128)S(1)} %fusion.19, pred[1536]{0:T(1024)(128)(4,1)S(1)} %iota_compare_fusion, bf16[1536,2,64]{0,2,1:T(8,128)(2,1)S(1)} %bitcast.37, bf16[1536,2,64]{0,2,1:T(8,128)(2,1)S(1)} %bitcast.39), kind=kOutput, calls=%fused_computation.12 | convolution fusion | flops 1231950336 | bytes 1586688 | tf_op jit(solution)/shard_map/hqk,khd->qhd/dot_general | solution.py:118
  97.3 0.9 copy.24
  (2 shorter events, 0.0 us)
Async XLA Ops:
  0.0 8.8 %copy-start = (bf16[1,192,8192]{2,1,0:T(8,128)(2,1)S(1)}, bf16[1,192,8192]{2,1,0:T(8,128)(2,1)}, u32[]{:S(2)}) copy-start(bf16[1,192,8192]{2,1,0:T(8,128)(2,1)} %param.7) | copy-start | bytes 9437188
  0.0 8.8 %copy-start.3 = (f32[256]{0:T(256)S(1)}, f32[256]{0:T(256)}, u32[]{:S(2)}) copy-start(f32[256]{0:T(256)} %param.10) | copy-start | bytes 3076
  0.0 8.8 %copy-start.2 = (f32[1024]{0:T(1024)S(1)}, f32[1024]{0:T(1024)}, u32[]{:S(2)}) copy-start(f32[1024]{0:T(1024)} %param.12) | copy-start | bytes 12292
  0.0 8.8 %copy-start.1 = (bf16[7,64,256]{2,1,0:T(8,128)(2,1)S(1)}, bf16[7,64,256]{2,1,0:T(8,128)(2,1)}, u32[]{:S(2)}) copy-start(bf16[7,64,256]{2,1,0:T(8,128)(2,1)} %w1_ref.1) | copy-start | bytes 688132
  8.8 45.9 %copy-start.4 = (bf16[1024,3,1024]{0,2,1:T(8,128)(2,1)S(1)}, bf16[1024,3,1024]{0,2,1:T(8,128)(2,1)}, u32[]{:S(2)}) copy-start(bf16[1024,3,1024]{0,2,1:T(8,128)(2,1)} %copy.17) | copy-start | bytes 18874372
  58.4 23.2 %all-to-all-start = ((bf16[192,3,8,128]{3,0,1,2:T(8,128)(2,1)}), bf16[192,3,8,128]{3,0,1,2:T(8,128)(2,1)S(1)}, u32[]{:S(2)}, u32[]{:S(2)}) async-start(bf16[192,3,8,128]{3,0,1,2:T(8,128)(2,1)} %copy.18), calls=%async_computation | async-start | bytes 2359296 | tf_op jit(solution)/shard_map/all_to_all | solution.py:103

commit v2 on v1

v2 whole, which is shorter than its diff:
```python
import functools

import jax
import jax.numpy as jnp
from jax import lax
from jax.experimental import pallas as pl
from jax.experimental.pallas import tpu as pltpu
from jax.sharding import PartitionSpec as P

HD = 64
ROOT = 0.7978845608028654
CUBE = ROOT * 0.044715
LOG2E = 1.4426950408889634
CHUNKS = 2
FRAMES_STEP = 8
PAIRS_STEP = 8
Q_ROWS = 256
F32 = jnp.float32
BF16 = jnp.bfloat16


def gelu_twice(y):
    return y + y * jnp.tanh(y * (ROOT + CUBE * (y * y)))


def dot(a, b):
    return jnp.dot(a, b, preferred_element_type=F32)


def first_layer(x_ref, rows, n, bias, w1p_ref, x0_ref, x1_ref, x2_ref, x3_ref, carry_ref):
    c1 = w1p_ref.shape[1]
    lane = w1p_ref.shape[0] // 4
    frames = x_ref.shape[1] // lane
    blank = jnp.zeros((n, c1), BF16)
    x0_ref[0, :, c1:] = blank
    x1_ref[0, :, c1:] = blank
    carry_ref[...] = jnp.zeros_like(carry_ref)

    def emit(p, even0, odd0, even1, odd1):
        before1, before0, odd_before = carry_ref[0], carry_ref[1], carry_ref[2]
        x0_ref[p, :, :c1] = (before1 - even1).astype(BF16)
        x1_ref[p, :, :c1] = (even0 + even1).astype(BF16)
        x2_ref[p] = (even1 - even0).astype(BF16)
        x3_ref[p, :, :c1] = (before0 - even0).astype(BF16)
        x0_ref[p + 1, :, c1:] = (odd0 - odd1).astype(BF16)
        x1_ref[p + 1, :, c1:] = odd1.astype(BF16)
        x3_ref[p, :, c1:] = (odd_before - odd0).astype(BF16)
        carry_ref[0] = even1
        carry_ref[1] = even0
        carry_ref[2] = odd1

    def act(y):
        return 0.5 * gelu_twice(y + bias)

    def piece(t):
        lo, hi = max(t - 2, 0), min(t + 2, frames)
        weight = w1p_ref[(lo - t + 2) * lane : (hi - t + 2) * lane, :]
        return act(dot(x_ref[rows, lo * lane : hi * lane], weight))

    def window(t):
        return x_ref[rows, pl.ds(pl.multiple_of((t - 2) * lane, lane), 4 * lane)]

    def many(p, count):
        lhs = jnp.concatenate([window(4 * p + j) for j in range(4 * count)], axis=0)
        y = act(dot(lhs, w1p_ref[...]))
        for q in range(count):
            emit(p + q, *[y[(4 * q + j) * n : (4 * q + j + 1) * n] for j in range(4)])

    per = FRAMES_STEP // 4
    quads = frames // 4
    emit(0, *[piece(j) for j in range(4)])

    def step(i, _):
        many(1 + i * per, per)
        return 0

    loops = (quads - 2) // per
    lax.fori_loop(0, loops, step, 0)
    for p in range(1 + loops * per, quads - 1):
        many(p, 1)
    emit(quads - 1, *[piece(frames - 4 + j) for j in range(4)])
    x3_ref[quads, :, :c1] = carry_ref[1].astype(BF16)
    x3_ref[quads, :, c1:] = carry_ref[2].astype(BF16)


def second_layer(n, bias_ref, wt_ref, x0_ref, x1_ref, x2_ref, x3_ref, part_ref, acc_ref):
    c1 = x2_ref.shape[2]
    width = wt_ref.shape[1]
    acc_ref[...] = jnp.zeros_like(acc_ref)

    def step(i, _):
        def rows_of(make):
            return jnp.concatenate([make(i * PAIRS_STEP + g) for g in range(PAIRS_STEP)], axis=0)

        lhs0 = rows_of(lambda p: jnp.concatenate([x0_ref[p], x0_ref[p + 1, :, c1:]], axis=1))
        lhs1 = rows_of(lambda p: jnp.concatenate([x1_ref[p], x1_ref[p + 1, :, c1:]], axis=1))
        lhs2 = rows_of(lambda p: x2_ref[p])
        lhs3 = rows_of(
            lambda p: jnp.concatenate(
                [x3_ref[p + 1, :, :c1], x3_ref[p, :, c1:], x3_ref[p + 1, :, c1:]], axis=1
            )
        )
        for block in range(width // c1):
            cols = slice(block * c1, (block + 1) * c1)
            slot = (block % 2) * 2
            part_ref[slot] = dot(lhs1, wt_ref[3 * c1 : 6 * c1, cols]) + bias_ref[:, cols]
            part_ref[slot + 1] = dot(lhs2, wt_ref[6 * c1 : 7 * c1, cols])
            y0 = dot(lhs0, wt_ref[0 : 3 * c1, cols]) + (part_ref[slot] + part_ref[slot + 1])
            y1 = (part_ref[slot] - part_ref[slot + 1]) - dot(lhs3, wt_ref[7 * c1 : 10 * c1, cols])
            y = gelu_twice(y0) + gelu_twice(y1)
            total = y[0:n]
            for g in range(1, PAIRS_STEP):
                total = total + y[g * n : (g + 1) * n]
            acc_ref[:, cols] += total
        return 0

    lax.fori_loop(0, x2_ref.shape[0] // PAIRS_STEP, step, 0)


def attend(count, q_ref, k_ref, v_ref, o_ref):
    slots, width = k_ref.shape
    k_row = lax.broadcasted_iota(jnp.int32, (slots, width), 0)
    k_lane = lax.broadcasted_iota(jnp.int32, (slots, width), 1)
    q_lane = lax.broadcasted_iota(jnp.int32, (Q_ROWS, width), 1)
    keys, values = [], []
    zero = jnp.zeros((), F32)
    for head in range(2):
        mine = (k_lane >= head * HD) & (k_lane < (head + 1) * HD)
        spare = k_lane == (HD if head == 0 else 0)
        bias = jnp.where(k_row < count, zero, F32(-1e30))
        keys.append(jnp.where(mine, k_ref[...].astype(F32), jnp.where(spare, bias, zero)).astype(BF16))
        values.append(
            jnp.where(mine, v_ref[...].astype(F32), jnp.where(spare, F32(1), zero)).astype(BF16)
        )

    for block in range(slots // Q_ROWS):
        rows = slice(block * Q_ROWS, (block + 1) * Q_ROWS)
        query = q_ref[rows, :].astype(F32)
        outs = []
        for head in range(2):
            mine = (q_lane >= head * HD) & (q_lane < (head + 1) * HD)
            at = HD if head == 0 else 0
            wide = jnp.where(mine, query, jnp.where(q_lane == at, F32(1), zero)).astype(BF16)
            scores = lax.dot_general(
                wide, keys[head], (((1,), (1,)), ((), ())), preferred_element_type=F32
            )
            top = jnp.max(scores, axis=1, keepdims=True)
            powered = jnp.exp2(scores - top).astype(BF16)
            summed = dot(powered, values[head])
            outs.append(summed / summed[:, at : at + 1])
        row = lax.broadcasted_iota(jnp.int32, (Q_ROWS, width), 0) + block * Q_ROWS
        out = jnp.where(q_lane < HD, outs[0], outs[1])
        o_ref[rows, :] = jnp.where(row < count, out, zero).astype(BF16)


def body(
    ring,
    count_ref, x_hbm, w1_ref, b1_ref, w2_hbm, b2_ref, proj_hbm,
    o_ref,
    x_ref, w1p_ref, wt_ref, mid_ref, proj_ref,
    x0_ref, x1_ref, x2_ref, x3_ref, carry_ref, part_ref, acc_ref,
    send_ref, got_ref,
    x_sem, w_sem, p_sem, send_sem, recv_sem,
):
    me = lax.axis_index("head")
    rec = lax.axis_index("rec")
    total_rows = x_ref.shape[0]
    n = total_rows // CHUNKS
    taps, c0, c1 = w1_ref.shape
    barrier = pltpu.get_barrier_semaphore()
    for i in range(1, ring):
        pl.semaphore_signal(
            barrier, inc=1, device_id=(rec, lax.rem(me + i, ring)),
            device_id_type=pl.DeviceIdType.MESH,
        )
    loads = [
        pltpu.make_async_copy(
            x_hbm.at[pl.ds(c * n, n)], x_ref.at[pl.ds(c * n, n)], x_sem.at[c]
        )
        for c in range(CHUNKS)
    ]
    place = {1: 0, 0: 1, 4: 2, 5: 7, 2: 8, 6: 9}
    weights = [
        pltpu.make_async_copy(
            w2_hbm.at[k],
            mid_ref if k == 3 else wt_ref.at[pl.ds(place[k] * c1, c1)],
            w_sem.at[k],
        )
        for k in range(taps)
    ]
    proj_load = pltpu.make_async_copy(proj_hbm, proj_ref, p_sem)
    loads[0].start()
    for w in weights:
        w.start()
    for load in loads[1:]:
        load.start()
    proj_load.start()
    w1p_ref[0:c0, :] = jnp.zeros((c0, c1), BF16)
    w1p_ref[c0:, :] = w1_ref[...].reshape(taps * c0, c1)
    bias = b1_ref[...]

    def sends(c):
        return [
            pltpu.make_async_remote_copy(
                src_ref=send_ref.at[lax.rem(me + i, ring), :, pl.ds(c * n, n)],
                dst_ref=got_ref.at[:, pl.ds(me * total_rows + c * n, n)],
                send_sem=send_sem.at[c, i - 1],
                recv_sem=recv_sem.at[c, i - 1],
                device_id=(rec, lax.rem(me + i, ring)),
                device_id_type=pl.DeviceIdType.MESH,
            )
            for i in range(1, ring)
        ]

    def chunk(c, _):
        start = pl.multiple_of(c * n, n)
        rows = pl.ds(start, n)
        pltpu.make_async_copy(x_hbm.at[rows], x_ref.at[rows], x_sem.at[c]).wait()
        first_layer(x_ref, rows, n, bias, w1p_ref, x0_ref, x1_ref, x2_ref, x3_ref, carry_ref)

        @pl.when(c == 0)
        def _():
            for w in weights:
                w.wait()

            def tap(k):
                if k == 3:
                    return mid_ref[...].astype(F32)
                return wt_ref[place[k] * c1 : (place[k] + 1) * c1, :].astype(F32)

            ends = tap(1) + tap(5)
            wt_ref[3 * c1 : 4 * c1, :] = (0.5 * (ends + tap(3))).astype(BF16)
            wt_ref[6 * c1 : 7 * c1, :] = (0.5 * (ends - tap(3))).astype(BF16)
            wt_ref[4 * c1 : 5 * c1, :] = (tap(0) + tap(2)).astype(BF16)
            wt_ref[5 * c1 : 6 * c1, :] = (tap(4) + tap(6)).astype(BF16)

        second_layer(n, b2_ref, wt_ref, x0_ref, x1_ref, x2_ref, x3_ref, part_ref, acc_ref)
        embedded = (acc_ref[...] * (0.25 / x2_ref.shape[0])).astype(BF16)

        @pl.when(c == 0)
        def _():
            proj_load.wait()
            pl.semaphore_wait(barrier, ring - 1)

        width = got_ref.shape[2]
        for j in range(3):
            mixed = dot(embedded, proj_ref[j])
            if j == 0:
                mixed = mixed * (LOG2E * HD**-0.5)
            mixed = mixed.astype(BF16)
            for peer in range(ring):
                send_ref[peer, j, rows, :] = mixed[:, peer * width : (peer + 1) * width]
        for copy in sends(c):
            copy.start()
        own = pl.ds(pl.multiple_of(me * total_rows + c * n, n), n)
        got_ref[:, own, :] = send_ref[me, :, rows, :]
        return 0

    lax.fori_loop(0, CHUNKS, chunk, 0)
    for c in range(CHUNKS):
        for copy in sends(c):
            copy.wait()
    attend(count_ref[0], got_ref.at[0], got_ref.at[1], got_ref.at[2], o_ref)


def shards(spectrogram, epoch_counts, conv_first, bias_first, conv_second, bias_second, projection):
    ring = lax.axis_size("head")
    x = spectrogram[0]
    rows, flat = x.shape
    n = rows // CHUNKS
    taps, c0, c1 = conv_first.shape
    width = conv_second.shape[2]
    pairs = flat // (8 * c0)
    group = width // ring
    vmem = pl.BlockSpec(memory_space=pltpu.VMEM)
    hbm = pl.BlockSpec(memory_space=pl.ANY)
    out = pl.pallas_call(
        functools.partial(body, ring),
        out_shape=jax.ShapeDtypeStruct((rows * ring, group), BF16),
        in_specs=[pl.BlockSpec(memory_space=pltpu.SMEM), hbm, vmem, vmem, hbm, vmem, hbm],
        out_specs=vmem,
        scratch_shapes=[
            pltpu.VMEM((rows, flat), BF16),
            pltpu.VMEM(((taps + 1) * c0, c1), BF16),
            pltpu.VMEM((10 * c1, width), BF16),
            pltpu.VMEM((c1, width), BF16),
            pltpu.VMEM((3, width, width), BF16),
            pltpu.VMEM((pairs + 1, n, 2 * c1), BF16),
            pltpu.VMEM((pairs + 1, n, 2 * c1), BF16),
            pltpu.VMEM((pairs, n, c1), BF16),
            pltpu.VMEM((pairs + 1, n, 2 * c1), BF16),
            pltpu.VMEM((3, n, c1), F32),
            pltpu.VMEM((4, PAIRS_STEP * n, c1), F32),
            pltpu.VMEM((n, width), F32),
            pltpu.VMEM((ring, 3, rows, group), BF16),
            pltpu.VMEM((3, rows * ring, group), BF16),
            pltpu.SemaphoreType.DMA((CHUNKS,)),
            pltpu.SemaphoreType.DMA((taps,)),
            pltpu.SemaphoreType.DMA,
            pltpu.SemaphoreType.DMA((CHUNKS, ring - 1)),
            pltpu.SemaphoreType.DMA((CHUNKS, ring - 1)),
        ],
        compiler_params=pltpu.CompilerParams(
            vmem_limit_bytes=56 * 1024 * 1024, collective_id=0, has_side_effects=True
        ),
        name="stem_attention",
    )(
        epoch_counts, x, conv_first, bias_first.reshape(1, -1), conv_second,
        bias_second.reshape(1, -1), jnp.transpose(projection, (1, 0, 2)),
    )
    return out[None]


def solution(mesh):
    return jax.shard_map(
        shards,
        mesh=mesh,
        in_specs=(P("rec", "head", None), P("rec"), P(), P(), P(), P(), P()),
        out_specs=P("rec", None, "head"),
        check_vma=False,
    )
```

time: 98.5 us -> 57 us (0.58)
  matrix products: 17.2 us -> 0 us
  waiting for transfers between devices: 15.9 us -> 0 us
  local copies, waits for them, and re-layouts: 11.9 us -> 1.77 us
  Pallas kernels: 45.8 us -> 54.5 us
  starting transfers between devices: 6.69 us -> 0 us
    all_to_all x1 -> x0, waiting for transfers between devices: 15.9 us -> none  [shards(): lax.all_to_all(mixed_rows, 'head', split_axis=2, concat_axis=0, tiled=True)]
    dot_general x2 -> x0, matrix products: 10.4 us -> none  [the longest x1 8.19 us: shards(): jnp.einsum('hqk,khd->qhd', probabilities, values, preferred_element_type=...]
    pallas_call x1, Pallas kernels: 45.8 us -> 54.5 us  [shards(): pl.pallas_call(functools.partial(body, ring), out_shape=jax.ShapeDtypeStr...]
    unnamed x12 -> x1, local copies, waits for them, and re-layouts: 9.02 us -> 1.77 us
    sub x1 -> x0, matrix products: 6.77 us -> none  [shards(): powered = jnp.exp(scores - row_max)]
    all_to_all x1 -> x0, starting transfers between devices: 6.69 us -> none  [shards(): lax.all_to_all(mixed_rows, 'head', split_axis=2, concat_axis=0, tiled=True)]
    reshape x1 -> x0, local copies, waits for them, and re-layouts: 1.27 us -> none  [shards(): mixed_rows = mixed_rows.reshape(slot_count, 3, heads_dev, group_width)]
  transfers between devices with their start and end apart: 1 -> 0, of which waited for: 1 -> 0; matrix products, arithmetic and copies ran while one was open for 0% -> 0% of each run, Pallas kernels for 0% -> 0%
where the time goes in v2:
time: 57 us; the launch traced here: 56.9 us
  Pallas kernels  54.5 us (96%)
  local copies, waits for them, and re-layouts  1.77 us (3%)
  between operations  0.66 us (1%)
    pallas_call x1, Pallas kernels, shards(): pl.pallas_call(functools.partial(body, ring), out_shape=jax.ShapeDtypeStr...  54.5 us
    unnamed x1, local copies, waits for them, and re-layouts  1.77 us

profile of v2, /device:TPU:1, one launch (start us, length us, event | category | flops | bytes accessed | tf_op | source)
XLA Modules:
  0.0 56.9 jit_solution(9808269125095688584)
XLA Ops:
  0.7 54.5 %stem_attention.1 = bf16[1536,128]{1,0:T(8,128)(2,1)} custom-call(s32[1]{0:T(128)S(6)} %copy.9.count_ref, bf16[192,8192]{1,0:T(8,128)(2,1)} %bitcast.6, bf16[7,64,256]{2,1,0:T(8,128)(2,1)} %w1_ref.1, f32[1,256]{1,0:T(1,128)} %bitcast.9, bf16[7,256,1024]{2,1,0:T(8,128)(2,1)} %w2_hbm.1, f32[1,1024]{1,0:T(1,128)} %bitcast.8, bf16[3,1024,1024]{2,1,0:T(8,128)(2,1)} %bitcast.5), custom_call_target="tpu_custom_call" | custom-call | tf_op jit(solution)/shard_map/stem_attention/pallas_call | solution.py:277
  55.1 1.8 %copy.10 = bf16[1,1536,128]{2,1,0:T(8,128)(2,1)} copy(bf16[1,1536,128]{2,1,0:T(8,128)(2,1)} %bitcast.7) | data formatting | bytes 786432

commit v3 on v2

--- a/solution.py
+++ b/solution.py
@@ -11,16 +11,24 @@
 ROOT = 0.7978845608028654
 CUBE = ROOT * 0.044715
 LOG2E = 1.4426950408889634
-CHUNKS = 2
-FRAMES_STEP = 8
-PAIRS_STEP = 8
-Q_ROWS = 256
+CHUNKS = 3
+FRAMES_STEP = 16
+PAIRS_STEP = 16
+Q_ROWS = 512
 F32 = jnp.float32
 BF16 = jnp.bfloat16
 
 
 def gelu_twice(y):
     return y + y * jnp.tanh(y * (ROOT + CUBE * (y * y)))
+
+
+def gelu_twice16(z):
+    return z + z * jnp.tanh(z * (BF16(ROOT) + BF16(CUBE) * (z * z)))
+
+
+def gelu_half(z):
+    return z + z * jnp.tanh(z * (BF16(2 * ROOT) + BF16(8 * CUBE) * (z * z)))
 
 
 def dot(a, b):
@@ -50,7 +58,7 @@
         carry_ref[2] = odd1
 
     def act(y):
-        return 0.5 * gelu_twice(y + bias)
+        return gelu_half((y + bias).astype(BF16))
 
     def piece(t):
         lo, hi = max(t - 2, 0), min(t + 2, frames)
@@ -76,8 +84,9 @@
 
     loops = (quads - 2) // per
     lax.fori_loop(0, loops, step, 0)
-    for p in range(1 + loops * per, quads - 1):
-        many(p, 1)
+    rest = quads - 1 - (1 + loops * per)
+    if rest:
+        many(1 + loops * per, rest)
     emit(quads - 1, *[piece(frames - 4 + j) for j in range(4)])
     x3_ref[quads, :, :c1] = carry_ref[1].astype(BF16)
     x3_ref[quads, :, c1:] = carry_ref[2].astype(BF16)
@@ -107,50 +116,97 @@
             part_ref[slot + 1] = dot(lhs2, wt_ref[6 * c1 : 7 * c1, cols])
             y0 = dot(lhs0, wt_ref[0 : 3 * c1, cols]) + (part_ref[slot] + part_ref[slot + 1])
             y1 = (part_ref[slot] - part_ref[slot + 1]) - dot(lhs3, wt_ref[7 * c1 : 10 * c1, cols])
-            y = gelu_twice(y0) + gelu_twice(y1)
-            total = y[0:n]
+            y = gelu_twice16(y0.astype(BF16)) + gelu_twice16(y1.astype(BF16))
+            total = y[0:n].astype(F32)
             for g in range(1, PAIRS_STEP):
-                total = total + y[g * n : (g + 1) * n]
+                total = total + y[g * n : (g + 1) * n].astype(F32)
             acc_ref[:, cols] += total
         return 0
 
     lax.fori_loop(0, x2_ref.shape[0] // PAIRS_STEP, step, 0)
 
 
-def attend(count, q_ref, k_ref, v_ref, o_ref):
-    slots, width = k_ref.shape
-    k_row = lax.broadcasted_iota(jnp.int32, (slots, width), 0)
-    k_lane = lax.broadcasted_iota(jnp.int32, (slots, width), 1)
-    q_lane = lax.broadcasted_iota(jnp.int32, (Q_ROWS, width), 1)
-    keys, values = [], []
+def attend_parts(count, got_a, got_b, part_a, part_b, rows_all, o_ref, base_ref, top_ref, kv_ref, between):
+    width = got_a.shape[2]
     zero = jnp.zeros((), F32)
-    for head in range(2):
-        mine = (k_lane >= head * HD) & (k_lane < (head + 1) * HD)
-        spare = k_lane == (HD if head == 0 else 0)
-        bias = jnp.where(k_row < count, zero, F32(-1e30))
-        keys.append(jnp.where(mine, k_ref[...].astype(F32), jnp.where(spare, bias, zero)).astype(BF16))
-        values.append(
-            jnp.where(mine, v_ref[...].astype(F32), jnp.where(spare, F32(1), zero)).astype(BF16)
-        )
-
-    for block in range(slots // Q_ROWS):
+
+    def slot_of(shape, offset, part, start):
+        row = lax.broadcasted_iota(jnp.int32, shape, 0) + offset
+        return lax.div(row, part) * rows_all + lax.rem(row, part) + start
+
+    def lanes(n, head):
+        lane = lax.broadcasted_iota(jnp.int32, (n, width), 1)
+        at = HD if head == 0 else 0
+        return (lane >= head * HD) & (lane < (head + 1) * HD), lane == at, at
+
+    def prepare(got, part, start, off):
+        n = got.shape[1]
+        live = slot_of((n, width), 0, part, start) < count
+        bias = jnp.where(live, zero, F32(-1e30))
+        for head in range(2):
+            mine, spare, _ = lanes(n, head)
+            kv_ref[head, off : off + n, :] = jnp.where(
+                mine, got[1].astype(F32), jnp.where(spare, bias, zero)
+            ).astype(BF16)
+            kv_ref[2 + head, off : off + n, :] = jnp.where(
+                mine, got[2].astype(F32), jnp.where(spare, F32(1), zero)
+            ).astype(BF16)
+
+    def query(got, block, head):
+        mine, spare, at = lanes(Q_ROWS, head)
+        q = got[0, block * Q_ROWS : (block + 1) * Q_ROWS, :].astype(F32)
+        return jnp.where(mine, q, jnp.where(spare, F32(1), zero)).astype(BF16), at
+
+    def score(wide, head, lo, hi):
+        return lax.dot_general(
+            wide, kv_ref[head, lo:hi, :], (((1,), (1,)), ((), ())), preferred_element_type=F32
+        )
+
+    def gather(scores, top, head, lo, hi):
+        return dot(jnp.exp2(scores - top).astype(BF16), kv_ref[2 + head, lo:hi, :])
+
+    def finish(outs, block, part, start):
+        lane = lax.broadcasted_iota(jnp.int32, (Q_ROWS, width), 1)
+        out = jnp.where(lane < HD, outs[0], outs[1])
+        live = slot_of((Q_ROWS, width), block * Q_ROWS, part, start) < count
+        out = jnp.where(live, out, zero).astype(BF16)
+        for k in range(Q_ROWS // part):
+            at = (block * (Q_ROWS // part) + k) * rows_all + start
+            o_ref[at : at + part, :] = out[k * part : (k + 1) * part]
+
+    na, nb = got_a.shape[1], got_b.shape[1]
+    prepare(got_a, part_a, 0, 0)
+    for block in range(na // Q_ROWS):
         rows = slice(block * Q_ROWS, (block + 1) * Q_ROWS)
-        query = q_ref[rows, :].astype(F32)
+        for head in range(2):
+            wide, _ = query(got_a, block, head)
+            scores = score(wide, head, 0, na)
+            top = jnp.max(scores, axis=1, keepdims=True)
+            top_ref[head, rows, :] = jnp.broadcast_to(top, (Q_ROWS, width))
+            base_ref[head, rows, :] = gather(scores, top, head, 0, na)
+    between()
+    prepare(got_b, part_b, part_a, na)
+    for block in range(na // Q_ROWS):
+        rows = slice(block * Q_ROWS, (block + 1) * Q_ROWS)
         outs = []
         for head in range(2):
-            mine = (q_lane >= head * HD) & (q_lane < (head + 1) * HD)
-            at = HD if head == 0 else 0
-            wide = jnp.where(mine, query, jnp.where(q_lane == at, F32(1), zero)).astype(BF16)
-            scores = lax.dot_general(
-                wide, keys[head], (((1,), (1,)), ((), ())), preferred_element_type=F32
-            )
+            wide, at = query(got_a, block, head)
+            scores = score(wide, head, na, na + nb)
+            before = top_ref[head, rows, 0:1]
+            top = jnp.maximum(before, jnp.max(scores, axis=1, keepdims=True))
+            summed = base_ref[head, rows, :] * jnp.exp2(before - top)
+            summed = summed + gather(scores, top, head, na, na + nb)
+            outs.append(summed / summed[:, at : at + 1])
+        finish(outs, block, part_a, 0)
+    for block in range(nb // Q_ROWS):
+        outs = []
+        for head in range(2):
+            wide, at = query(got_b, block, head)
+            scores = score(wide, head, 0, na + nb)
             top = jnp.max(scores, axis=1, keepdims=True)
-            powered = jnp.exp2(scores - top).astype(BF16)
-            summed = dot(powered, values[head])
+            summed = gather(scores, top, head, 0, na + nb)
             outs.append(summed / summed[:, at : at + 1])
-        row = lax.broadcasted_iota(jnp.int32, (Q_ROWS, width), 0) + block * Q_ROWS
-        out = jnp.where(q_lane < HD, outs[0], outs[1])
-        o_ref[rows, :] = jnp.where(row < count, out, zero).astype(BF16)
+        finish(outs, block, part_b, part_a)
 
 
 def body(
@@ -158,8 +214,8 @@
     count_ref, x_hbm, w1_ref, b1_ref, w2_hbm, b2_ref, proj_hbm,
     o_ref,
     x_ref, w1p_ref, wt_ref, mid_ref, proj_ref,
-    x0_ref, x1_ref, x2_ref, x3_ref, carry_ref, part_ref, acc_ref,
-    send_ref, got_ref,
+    x0_ref, x1_ref, x2_ref, x3_ref, carry_ref, part_ref, acc_ref, emb_ref,
+    send_a, send_b, got_a, got_b, base_ref, top_ref, kv_ref,
     x_sem, w_sem, p_sem, send_sem, recv_sem,
 ):
     me = lax.axis_index("head")
@@ -196,22 +252,41 @@
         load.start()
     proj_load.start()
     w1p_ref[0:c0, :] = jnp.zeros((c0, c1), BF16)
-    w1p_ref[c0:, :] = w1_ref[...].reshape(taps * c0, c1)
-    bias = b1_ref[...]
-
-    def sends(c):
+    w1p_ref[c0:, :] = w1_ref[...].reshape(taps * c0, c1) * BF16(0.5)
+    bias = b1_ref[...] * 0.5
+
+    part_b = n
+    part_a = total_rows - n
+    groups = [(0, send_a, got_a, part_a, 0), (1, send_b, got_b, part_b, part_a)]
+
+    def sends(group):
+        g, src, dst, part, _ = group
         return [
             pltpu.make_async_remote_copy(
-                src_ref=send_ref.at[lax.rem(me + i, ring), :, pl.ds(c * n, n)],
-                dst_ref=got_ref.at[:, pl.ds(me * total_rows + c * n, n)],
-                send_sem=send_sem.at[c, i - 1],
-                recv_sem=recv_sem.at[c, i - 1],
+                src_ref=src.at[lax.rem(me + i, ring)],
+                dst_ref=dst.at[:, pl.ds(pl.multiple_of(me * part, part), part)],
+                send_sem=send_sem.at[g, i - 1],
+                recv_sem=recv_sem.at[g, i - 1],
                 device_id=(rec, lax.rem(me + i, ring)),
                 device_id_type=pl.DeviceIdType.MESH,
             )
             for i in range(1, ring)
         ]
 
+    def project(group):
+        g, src, dst, part, start = group
+        width = dst.shape[2]
+        for j in range(3):
+            mixed = dot(emb_ref[start : start + part, :], proj_ref[j])
+            if j == 0:
+                mixed = mixed * (LOG2E * HD**-0.5)
+            mixed = mixed.astype(BF16)
+            for peer in range(ring):
+                src[peer, j] = mixed[:, peer * width : (peer + 1) * width]
+        for copy in sends(group):
+            copy.start()
+        dst[:, pl.ds(pl.multiple_of(me * part, part), part), :] = src[me]
+
     def chunk(c, _):
         start = pl.multiple_of(c * n, n)
         rows = pl.ds(start, n)
@@ -235,32 +310,28 @@
             wt_ref[5 * c1 : 6 * c1, :] = (tap(4) + tap(6)).astype(BF16)
 
         second_layer(n, b2_ref, wt_ref, x0_ref, x1_ref, x2_ref, x3_ref, part_ref, acc_ref)
-        embedded = (acc_ref[...] * (0.25 / x2_ref.shape[0])).astype(BF16)
-
-        @pl.when(c == 0)
+        emb_ref[rows, :] = (acc_ref[...] * (0.25 / x2_ref.shape[0])).astype(BF16)
+
+        @pl.when(c == CHUNKS - 2)
         def _():
             proj_load.wait()
             pl.semaphore_wait(barrier, ring - 1)
-
-        width = got_ref.shape[2]
-        for j in range(3):
-            mixed = dot(embedded, proj_ref[j])
-            if j == 0:
-                mixed = mixed * (LOG2E * HD**-0.5)
-            mixed = mixed.astype(BF16)
-            for peer in range(ring):
-                send_ref[peer, j, rows, :] = mixed[:, peer * width : (peer + 1) * width]
-        for copy in sends(c):
-            copy.start()
-        own = pl.ds(pl.multiple_of(me * total_rows + c * n, n), n)
-        got_ref[:, own, :] = send_ref[me, :, rows, :]
+            project(groups[0])
+
         return 0
 
     lax.fori_loop(0, CHUNKS, chunk, 0)
-    for c in range(CHUNKS):
-        for copy in sends(c):
+    project(groups[1])
+    for copy in sends(groups[0]):
+        copy.wait()
+
+    def between():
+        for copy in sends(groups[1]):
             copy.wait()
-    attend(count_ref[0], got_ref.at[0], got_ref.at[1], got_ref.at[2], o_ref)
+
+    attend_parts(
+        count_ref[0], got_a, got_b, part_a, part_b, total_rows, o_ref, base_ref, top_ref, kv_ref, between
+    )
 
 
 def shards(spectrogram, epoch_counts, conv_first, bias_first, conv_second, bias_second, projection):
@@ -289,16 +360,22 @@
             pltpu.VMEM((pairs + 1, n, 2 * c1), BF16),
             pltpu.VMEM((pairs, n, c1), BF16),
             pltpu.VMEM((pairs + 1, n, 2 * c1), BF16),
-            pltpu.VMEM((3, n, c1), F32),
+            pltpu.VMEM((3, n, c1), BF16),
             pltpu.VMEM((4, PAIRS_STEP * n, c1), F32),
             pltpu.VMEM((n, width), F32),
-            pltpu.VMEM((ring, 3, rows, group), BF16),
-            pltpu.VMEM((3, rows * ring, group), BF16),
+            pltpu.VMEM((rows, width), BF16),
+            pltpu.VMEM((ring, 3, rows - n, group), BF16),
+            pltpu.VMEM((ring, 3, n, group), BF16),
+            pltpu.VMEM((3, (rows - n) * ring, group), BF16),
+            pltpu.VMEM((3, n * ring, group), BF16),
+            pltpu.VMEM((2, (rows - n) * ring, group), F32),
+            pltpu.VMEM((2, (rows - n) * ring, group), F32),
+            pltpu.VMEM((4, rows * ring, group), BF16),
             pltpu.SemaphoreType.DMA((CHUNKS,)),
             pltpu.SemaphoreType.DMA((taps,)),
             pltpu.SemaphoreType.DMA,
-            pltpu.SemaphoreType.DMA((CHUNKS, ring - 1)),
-            pltpu.SemaphoreType.DMA((CHUNKS, ring - 1)),
+            pltpu.SemaphoreType.DMA((2, ring - 1)),
+            pltpu.SemaphoreType.DMA((2, ring - 1)),
         ],
         compiler_params=pltpu.CompilerParams(
             vmem_limit_bytes=56 * 1024 * 1024, collective_id=0, has_side_effects=True

time: 57 us -> 49 us (0.86)
  Pallas kernels: 54.5 us -> 46.5 us
    pallas_call x1, Pallas kernels: 54.5 us -> 46.5 us  [shards(): pl.pallas_call(functools.partial(body, ring), out_shape=jax.ShapeDtypeStr...]
where the time goes in v3:
time: 49 us; the launch traced here: 48.9 us
  Pallas kernels  46.5 us (95%)
  local copies, waits for them, and re-layouts  1.77 us (4%)
  between operations  0.66 us (1%)
    pallas_call x1, Pallas kernels, shards(): pl.pallas_call(functools.partial(body, ring), out_shape=jax.ShapeDtypeStr...  46.5 us
    unnamed x1, local copies, waits for them, and re-layouts  1.77 us

profile of v3, /device:TPU:1, one launch (start us, length us, event | category | flops | bytes accessed | tf_op | source)
XLA Modules:
  0.0 48.9 jit_solution(1046173982811547462)
XLA Ops:
  0.7 46.5 %stem_attention.1 = bf16[1536,128]{1,0:T(8,128)(2,1)} custom-call(s32[1]{0:T(128)S(6)} %copy.9.count_ref, bf16[192,8192]{1,0:T(8,128)(2,1)} %bitcast.6, bf16[7,64,256]{2,1,0:T(8,128)(2,1)} %w1_ref.1, f32[1,256]{1,0:T(1,128)} %bitcast.9, bf16[7,256,1024]{2,1,0:T(8,128)(2,1)} %w2_hbm.1, f32[1,1024]{1,0:T(1,128)} %bitcast.8, bf16[3,1024,1024]{2,1,0:T(8,128)(2,1)} %bitcast.5), custom_call_target="tpu_custom_call" | custom-call | tf_op jit(solution)/shard_map/stem_attention/pallas_call | solution.py:348
  47.1 1.8 %copy.10 = bf16[1,1536,128]{2,1,0:T(8,128)(2,1)} copy(bf16[1,1536,128]{2,1,0:T(8,128)(2,1)} %bitcast.7) | data formatting | bytes 786432

commit v4 on v3

v4 whole, which is shorter than its diff:
```python
import functools

import jax
import jax.numpy as jnp
from jax import lax
from jax.experimental import pallas as pl
from jax.experimental.pallas import tpu as pltpu
from jax.sharding import PartitionSpec as P

HD = 64
ROOT = 0.7978845608028654
CUBE = ROOT * 0.044715
LOG2E = 1.4426950408889634
CHUNKS = 3
PARTS = 4
Q_ROWS = 512
F32 = jnp.float32
BF16 = jnp.bfloat16


def gelu_twice(y):
    return y + y * jnp.tanh(y * (ROOT + CUBE * (y * y)))


def gelu_twice16(z):
    return z + z * jnp.tanh(z * (BF16(ROOT) + BF16(CUBE) * (z * z)))


def gelu_half(z):
    return z + z * jnp.tanh(z * (BF16(2 * ROOT) + BF16(8 * CUBE) * (z * z)))


def dot(a, b):
    return jnp.dot(a, b, preferred_element_type=F32)


def first_parts(x_ref, start, n, bias, w1p_ref, xs, carry_ref):
    x0_ref, x1_ref, x2_ref, x3_ref = xs
    c1 = w1p_ref.shape[1]
    lane = w1p_ref.shape[0] // 4
    quads = x2_ref.shape[0]
    per = quads // PARTS

    def emit(p, even0, odd0, even1, odd1):
        before1, before0, odd_before = carry_ref[0], carry_ref[1], carry_ref[2]
        x0_ref[p, :, :c1] = before1 - even1
        x1_ref[p, :, :c1] = even0 + even1
        x2_ref[p] = even1 - even0
        x3_ref[p, :, :c1] = before0 - even0
        x0_ref[p + 1, :, c1:] = odd0 - odd1
        x1_ref[p + 1, :, c1:] = odd1
        x3_ref[p, :, c1:] = odd_before - odd0
        carry_ref[0] = even1
        carry_ref[1] = even0
        carry_ref[2] = odd1

    def part(k):
        if k == 0:
            blank = jnp.zeros((n, c1), BF16)
            x0_ref[0, :, c1:] = blank
            x1_ref[0, :, c1:] = blank
            carry_ref[...] = jnp.zeros_like(carry_ref)
        first = 4 * per * k
        lhs = jnp.concatenate(
            [x_ref[start : start + n, (first + j) * lane : (first + j + 4) * lane] for j in range(4 * per)],
            axis=0,
        )
        y = gelu_half((dot(lhs, w1p_ref[...]) + bias).astype(BF16))
        for q in range(per):
            emit(per * k + q, *[y[(4 * q + j) * n : (4 * q + j + 1) * n] for j in range(4)])
        if k == PARTS - 1:
            x3_ref[quads, :, :c1] = carry_ref[1]
            x3_ref[quads, :, c1:] = carry_ref[2]

    return part


def second_layer(n, bias_ref, wt_ref, xs, part_ref, emb_ref, start, weave):
    x0_ref, x1_ref, x2_ref, x3_ref = xs
    c1 = x2_ref.shape[2]
    pairs = x2_ref.shape[0]
    width = wt_ref.shape[1]

    def rows_of(make):
        return jnp.concatenate([make(p) for p in range(pairs)], axis=0)

    lhs0 = rows_of(lambda p: jnp.concatenate([x0_ref[p], x0_ref[p + 1, :, c1:]], axis=1))
    lhs1 = rows_of(lambda p: jnp.concatenate([x1_ref[p], x1_ref[p + 1, :, c1:]], axis=1))
    lhs2 = rows_of(lambda p: x2_ref[p])
    lhs3 = rows_of(
        lambda p: jnp.concatenate(
            [x3_ref[p + 1, :, :c1], x3_ref[p, :, c1:], x3_ref[p + 1, :, c1:]], axis=1
        )
    )
    for block in range(width // c1):
        cols = slice(block * c1, (block + 1) * c1)
        slot = (block % 2) * 2
        weave(block)
        part_ref[slot] = dot(lhs1, wt_ref[3 * c1 : 6 * c1, cols]) + bias_ref[:, cols]
        part_ref[slot + 1] = dot(lhs2, wt_ref[6 * c1 : 7 * c1, cols])
        y0 = dot(lhs0, wt_ref[0 : 3 * c1, cols]) + (part_ref[slot] + part_ref[slot + 1])
        y1 = (part_ref[slot] - part_ref[slot + 1]) - dot(lhs3, wt_ref[7 * c1 : 10 * c1, cols])
        y = gelu_twice16(y0.astype(BF16)) + gelu_twice16(y1.astype(BF16))
        total = y[0:n].astype(F32)
        for g in range(1, pairs):
            total = total + y[g * n : (g + 1) * n].astype(F32)
        emb_ref[start : start + n, cols] = (total * (0.25 / pairs)).astype(BF16)


def attend_parts(count, got_a, got_b, part_a, part_b, rows_all, o_ref, base_ref, top_ref, kv_ref, between):
    width = got_a.shape[2]
    zero = jnp.zeros((), F32)

    def slot_of(shape, offset, part, start):
        row = lax.broadcasted_iota(jnp.int32, shape, 0) + offset
        return lax.div(row, part) * rows_all + lax.rem(row, part) + start

    def lanes(n, head):
        lane = lax.broadcasted_iota(jnp.int32, (n, width), 1)
        at = HD if head == 0 else 0
        return (lane >= head * HD) & (lane < (head + 1) * HD), lane == at, at

    def prepare(got, part, start, off):
        n = got.shape[1]
        live = slot_of((n, width), 0, part, start) < count
        bias = jnp.where(live, zero, F32(-1e30))
        for head in range(2):
            mine, spare, _ = lanes(n, head)
            kv_ref[head, off : off + n, :] = jnp.where(
                mine, got[1].astype(F32), jnp.where(spare, bias, zero)
            ).astype(BF16)
            kv_ref[2 + head, off : off + n, :] = jnp.where(
                mine, got[2].astype(F32), jnp.where(spare, F32(1), zero)
            ).astype(BF16)

    def query(got, block, head):
        mine, spare, at = lanes(Q_ROWS, head)
        q = got[0, block * Q_ROWS : (block + 1) * Q_ROWS, :].astype(F32)
        return jnp.where(mine, q, jnp.where(spare, F32(1), zero)).astype(BF16), at

    def score(wide, head, lo, hi):
        return lax.dot_general(
            wide, kv_ref[head, lo:hi, :], (((1,), (1,)), ((), ())), preferred_element_type=F32
        )

    def gather(scores, top, head, lo, hi):
        return dot(jnp.exp2(scores - top).astype(BF16), kv_ref[2 + head, lo:hi, :])

    def finish(outs, block, part, start):
        lane = lax.broadcasted_iota(jnp.int32, (Q_ROWS, width), 1)
        out = jnp.where(lane < HD, outs[0], outs[1])
        out = out.astype(BF16)
        for k in range(Q_ROWS // part):
            at = (block * (Q_ROWS // part) + k) * rows_all + start
            o_ref[at : at + part, :] = out[k * part : (k + 1) * part]

    def ahead(tasks, scored, rest):
        current = scored(*tasks[0])
        for i, task in enumerate(tasks):
            upcoming = scored(*tasks[i + 1]) if i + 1 < len(tasks) else None
            rest(task, current)
            current = upcoming

    na, nb = got_a.shape[1], got_b.shape[1]
    prepare(got_a, part_a, 0, 0)

    def scored_first(block, head):
        return score(query(got_a, block, head)[0], head, 0, na)

    def rest_first(task, scores):
        block, head = task
        rows = slice(block * Q_ROWS, (block + 1) * Q_ROWS)
        top = jnp.max(scores, axis=1, keepdims=True)
        top_ref[head, rows, :] = jnp.broadcast_to(top, (Q_ROWS, width))
        base_ref[head, rows, :] = gather(scores, top, head, 0, na)

    ahead([(b, h) for b in range(na // Q_ROWS) for h in range(2)], scored_first, rest_first)
    between()
    prepare(got_b, part_b, part_a, na)
    kept = {}

    def scored_second(second, block, head):
        if second:
            return score(query(got_b, block, head)[0], head, 0, na + nb)
        return score(query(got_a, block, head)[0], head, na, na + nb)

    def rest_second(task, scores):
        second, block, head = task
        at = HD if head == 0 else 0
        rows = slice(block * Q_ROWS, (block + 1) * Q_ROWS)
        top = jnp.max(scores, axis=1, keepdims=True)
        if second:
            summed = gather(scores, top, head, 0, na + nb)
        else:
            before = top_ref[head, rows, 0:1]
            top = jnp.maximum(before, top)
            summed = base_ref[head, rows, :] * jnp.exp2(before - top)
            summed = summed + gather(scores, top, head, na, na + nb)
        kept[head] = summed / summed[:, at : at + 1]
        if head == 1:
            finish([kept[0], kept[1]], block, part_b if second else part_a, part_a if second else 0)

    ahead(
        [(g, b, h) for g, n in ((0, na), (1, nb)) for b in range(n // Q_ROWS) for h in range(2)],
        scored_second,
        rest_second,
    )


def body(
    ring,
    count_ref, x_hbm, w1_hbm, b1_hbm, w2_hbm, b2_hbm, proj_hbm,
    o_ref,
    x_ref, w1p_ref, b1_ref, b2_ref, wt_ref, mid_ref, proj_ref,
    xs_even, xs_odd, carry_ref, part_ref, emb_ref,
    send_a, send_b, got_a, got_b, base_ref, top_ref, kv_ref,
    x_sem, s_sem, w_sem, p_sem, send_sem, recv_sem,
):
    me = lax.axis_index("head")
    rec = lax.axis_index("rec")
    total_rows = x_ref.shape[0]
    n = total_rows // CHUNKS
    taps = w2_hbm.shape[0]
    wide, c1 = w1p_ref.shape
    c0 = wide // (taps + 1)
    barrier = pltpu.get_barrier_semaphore()
    for i in range(1, ring):
        pl.semaphore_signal(
            barrier, inc=1, device_id=(rec, lax.rem(me + i, ring)),
            device_id_type=pl.DeviceIdType.MESH,
        )
    loads = [
        pltpu.make_async_copy(
            x_hbm.at[pl.ds(c * n, n)],
            x_ref.at[pl.ds(c * n, n), pl.ds(4 * c0, x_hbm.shape[1])],
            x_sem.at[c],
        )
        for c in range(CHUNKS)
    ]
    place = {1: 0, 0: 1, 4: 2, 5: 7, 2: 8, 6: 9}
    weights = [
        pltpu.make_async_copy(
            w2_hbm.at[k],
            mid_ref if k == 3 else wt_ref.at[pl.ds(place[k] * c1, c1)],
            w_sem.at[k],
        )
        for k in range(taps)
    ]
    proj_load = pltpu.make_async_copy(proj_hbm, proj_ref, p_sem)
    small = [
        pltpu.make_async_copy(w1_hbm, w1p_ref.at[pl.ds(c0, taps * c0)], s_sem.at[0]),
        pltpu.make_async_copy(b1_hbm, b1_ref, s_sem.at[1]),
        pltpu.make_async_copy(b2_hbm, b2_ref, s_sem.at[2]),
    ]
    for load in small:
        load.start()
    loads[0].start()
    for w in weights:
        w.start()
    for load in loads[1:]:
        load.start()
    proj_load.start()
    x_ref[:, 0 : 4 * c0] = jnp.zeros((total_rows, 4 * c0), BF16)
    x_ref[:, 4 * c0 + x_hbm.shape[1] :] = jnp.zeros((total_rows, 2 * c0), BF16)
    w1p_ref[0:c0, :] = jnp.zeros((c0, c1), BF16)
    for load in small:
        load.wait()
    w1p_ref[c0:, :] = w1p_ref[c0:, :] * BF16(0.5)
    bias = b1_ref[...] * 0.5

    part_b = n
    part_a = total_rows - n
    groups = [(0, send_a, got_a, part_a, 0), (1, send_b, got_b, part_b, part_a)]

    def sends(group):
        g, src, dst, part, _ = group
        return [
            pltpu.make_async_remote_copy(
                src_ref=src.at[lax.rem(me + i, ring)],
                dst_ref=dst.at[:, pl.ds(pl.multiple_of(me * part, part), part)],
                send_sem=send_sem.at[g, i - 1],
                recv_sem=recv_sem.at[g, i - 1],
                device_id=(rec, lax.rem(me + i, ring)),
                device_id_type=pl.DeviceIdType.MESH,
            )
            for i in range(1, ring)
        ]

    def project(group):
        g, src, dst, part, start = group
        width = dst.shape[2]
        for j in range(3):
            mixed = dot(emb_ref[start : start + part, :], proj_ref[j])
            if j == 0:
                mixed = mixed * (LOG2E * HD**-0.5)
            mixed = mixed.astype(BF16)
            for peer in range(ring):
                src[peer, j] = mixed[:, peer * width : (peer + 1) * width]
        for copy in sends(group):
            copy.start()
        dst[:, pl.ds(pl.multiple_of(me * part, part), part), :] = src[me]

    xs = (xs_even, xs_odd)

    def parts_of(c):
        return first_parts(x_ref, c * n, n, bias, w1p_ref, xs[c % 2], carry_ref)

    loads[0].wait()
    for k in range(PARTS):
        parts_of(0)(k)
    for w in weights:
        w.wait()

    def tap(k):
        if k == 3:
            return mid_ref[...]
        return wt_ref[place[k] * c1 : (place[k] + 1) * c1, :]

    wt_ref[4 * c1 : 5 * c1, :] = tap(0) + tap(2)
    wt_ref[5 * c1 : 6 * c1, :] = tap(4) + tap(6)
    ends = tap(1).astype(F32) + tap(5).astype(F32)
    middle = tap(3).astype(F32)
    wt_ref[3 * c1 : 4 * c1, :] = (0.5 * (ends + middle)).astype(BF16)
    wt_ref[6 * c1 : 7 * c1, :] = (0.5 * (ends - middle)).astype(BF16)
    for c in range(CHUNKS):
        if c + 1 < CHUNKS:
            loads[c + 1].wait()
            weave = parts_of(c + 1)
        else:
            weave = lambda k: None
        second_layer(n, b2_ref, wt_ref, xs[c % 2], part_ref, emb_ref, c * n, weave)
        if c == CHUNKS - 2:
            proj_load.wait()
            pl.semaphore_wait(barrier, ring - 1)
            project(groups[0])
    project(groups[1])
    for copy in sends(groups[0]):
        copy.wait()

    def between():
        for copy in sends(groups[1]):
            copy.wait()

    attend_parts(
        count_ref[0], got_a, got_b, part_a, part_b, total_rows, o_ref, base_ref, top_ref, kv_ref, between
    )


def shards(spectrogram, epoch_counts, conv_first, bias_first, conv_second, bias_second, projection):
    ring = lax.axis_size("head")
    x = spectrogram[0]
    rows, flat = x.shape
    n = rows // CHUNKS
    taps, c0, c1 = conv_first.shape
    width = conv_second.shape[2]
    pairs = flat // (8 * c0)
    group = width // ring
    stage = (
        pltpu.VMEM((pairs + 1, n, 2 * c1), BF16),
        pltpu.VMEM((pairs + 1, n, 2 * c1), BF16),
        pltpu.VMEM((pairs, n, c1), BF16),
        pltpu.VMEM((pairs + 1, n, 2 * c1), BF16),
    )
    vmem = pl.BlockSpec(memory_space=pltpu.VMEM)
    hbm = pl.BlockSpec(memory_space=pltpu.HBM)
    out = pl.pallas_call(
        functools.partial(body, ring),
        out_shape=jax.ShapeDtypeStruct((rows * ring, group), BF16),
        in_specs=[pl.BlockSpec(memory_space=pltpu.SMEM), hbm, hbm, hbm, hbm, hbm, hbm],
        out_specs=vmem,
        scratch_shapes=[
            pltpu.VMEM((rows, flat + 6 * c0), BF16),
            pltpu.VMEM(((taps + 1) * c0, c1), BF16),
            pltpu.VMEM((1, c1), F32),
            pltpu.VMEM((1, width), F32),
            pltpu.VMEM((10 * c1, width), BF16),
            pltpu.VMEM((c1, width), BF16),
            pltpu.VMEM((3, width, width), BF16),
            stage,
            stage,
            pltpu.VMEM((3, n, c1), BF16),
            pltpu.VMEM((4, pairs * n, c1), F32),
            pltpu.VMEM((rows, width), BF16),
            pltpu.VMEM((ring, 3, rows - n, group), BF16),
            pltpu.VMEM((ring, 3, n, group), BF16),
            pltpu.VMEM((3, (rows - n) * ring, group), BF16),
            pltpu.VMEM((3, n * ring, group), BF16),
            pltpu.VMEM((2, (rows - n) * ring, group), F32),
            pltpu.VMEM((2, (rows - n) * ring, group), F32),
            pltpu.VMEM((4, rows * ring, group), BF16),
            pltpu.SemaphoreType.DMA((CHUNKS,)),
            pltpu.SemaphoreType.DMA((3,)),
            pltpu.SemaphoreType.DMA((taps,)),
            pltpu.SemaphoreType.DMA,
            pltpu.SemaphoreType.DMA((2, ring - 1)),
            pltpu.SemaphoreType.DMA((2, ring - 1)),
        ],
        compiler_params=pltpu.CompilerParams(
            vmem_limit_bytes=52 * 1024 * 1024, collective_id=0, has_side_effects=True
        ),
        name="stem_attention",
    )(
        epoch_counts,
        *[
            pltpu.with_memory_space_constraint(v, pltpu.HBM)
            for v in (
                x, conv_first.reshape(taps * c0, c1), bias_first.reshape(1, -1), conv_second,
                bias_second.reshape(1, -1), jnp.transpose(projection, (1, 0, 2)),
            )
        ],
    )
    live = jnp.arange(out.shape[0], dtype=jnp.int32) < epoch_counts[0]
    return jnp.where(live[:, None], out, jnp.zeros_like(out))[None]


def solution(mesh):
    return jax.shard_map(
        shards,
        mesh=mesh,
        in_specs=(P("rec", "head", None), P("rec"), P(), P(), P(), P(), P()),
        out_specs=P("rec", None, "head"),
        check_vma=False,
    )
```

time: 49 us -> 44.2 us (0.902)
  Pallas kernels: 46.5 us -> 42.5 us
  local copies, waits for them, and re-layouts: 1.77 us -> 0 us
  other arithmetic: 0 us -> 1.03 us
    pallas_call x1, Pallas kernels: 46.5 us -> 42.5 us  [shards(): pl.pallas_call(functools.partial(body, ring), out_shape=jax.ShapeDtypeStr...]
    unnamed x1 -> x0, local copies, waits for them, and re-layouts: 1.77 us -> none
    broadcast_in_dim x0 -> x1, other arithmetic: none -> 1.02 us  [shards(): return jnp.where(live[:, None], out, jnp.zeros_like(out))[None]]
where the time goes in v4:
time: 44.2 us
  Pallas kernels  42.5 us (96%)
  other arithmetic  1.03 us (2%)
  between operations  0.67 us (2%)
    pallas_call x1, Pallas kernels, shards(): pl.pallas_call(functools.partial(body, ring), out_shape=jax.ShapeDtypeStr...  42.5 us
    broadcast_in_dim x1, other arithmetic, shards(): return jnp.where(live[:, None], out, jnp.zeros_like(out))[None]  1.02 us

profile of v4, /device:TPU:1, one launch (start us, length us, event | category | flops | bytes accessed | tf_op | source)
XLA Modules:
  0.0 44.2 jit_solution(7162705495475399441)
XLA Ops:
  0.7 42.5 %stem_attention.1 = bf16[1536,128]{1,0:T(8,128)(2,1)S(1)} custom-call(s32[1]{0:T(128)} %copy.8.count_ref, bf16[192,8192]{1,0:T(8,128)(2,1)} %bitcast.10, bf16[448,256]{1,0:T(8,128)(2,1)} %bitcast.11, f32[1,256]{1,0:T(1,128)} %bitcast.13, bf16[7,256,1024]{2,1,0:T(8,128)(2,1)} %w2_hbm.1, f32[1,1024]{1,0:T(1,128)} %bitcast.12, bf16[3,1024,1024]{2,1,0:T(8,128)(2,1)} %bitcast.9), custom_call_target="tpu_custom_call" | custom-call | tf_op jit(solution)/shard_map/stem_attention/pallas_call | solution.py:366
  43.1 1.0 %select_bitcast_fusion = bf16[1,1536,128]{2,1,0:T(8,128)(2,1)} fusion(bf16[1536,128]{1,0:T(8,128)(2,1)S(1)} %stem_attention.1, pred[1536]{0:T(1024)(128)(4,1)S(1)} %iota_compare_fusion), kind=kLoop, calls=%fused_computation | loop fusion | flops 196608 | bytes 787968 | tf_op jit(solution)/shard_map/broadcast_in_dim | solution.py:413
  (1 shorter events, 0.0 us)

commit v5 on v4

--- a/solution.py
+++ b/solution.py
@@ -92,19 +92,31 @@
             [x3_ref[p + 1, :, :c1], x3_ref[p, :, c1:], x3_ref[p + 1, :, c1:]], axis=1
         )
     )
-    for block in range(width // c1):
+    blocks = width // c1
+
+    def products(block):
         cols = slice(block * c1, (block + 1) * c1)
         slot = (block % 2) * 2
-        weave(block)
         part_ref[slot] = dot(lhs1, wt_ref[3 * c1 : 6 * c1, cols]) + bias_ref[:, cols]
         part_ref[slot + 1] = dot(lhs2, wt_ref[6 * c1 : 7 * c1, cols])
         y0 = dot(lhs0, wt_ref[0 : 3 * c1, cols]) + (part_ref[slot] + part_ref[slot + 1])
         y1 = (part_ref[slot] - part_ref[slot + 1]) - dot(lhs3, wt_ref[7 * c1 : 10 * c1, cols])
-        y = gelu_twice16(y0.astype(BF16)) + gelu_twice16(y1.astype(BF16))
+        return y0.astype(BF16), y1.astype(BF16)
+
+    weave(0)
+    current = products(0)
+    for block in range(blocks):
+        upcoming = None
+        if block + 1 < blocks:
+            weave(block + 1)
+            upcoming = products(block + 1)
+        y = gelu_twice16(current[0]) + gelu_twice16(current[1])
         total = y[0:n].astype(F32)
         for g in range(1, pairs):
             total = total + y[g * n : (g + 1) * n].astype(F32)
+        cols = slice(block * c1, (block + 1) * c1)
         emb_ref[start : start + n, cols] = (total * (0.25 / pairs)).astype(BF16)
+        current = upcoming
 
 
 def attend_parts(count, got_a, got_b, part_a, part_b, rows_all, o_ref, base_ref, top_ref, kv_ref, between):
@@ -257,9 +269,6 @@
     loads[0].start()
     for w in weights:
         w.start()
-    for load in loads[1:]:
-        load.start()
-    proj_load.start()
     x_ref[:, 0 : 4 * c0] = jnp.zeros((total_rows, 4 * c0), BF16)
     x_ref[:, 4 * c0 + x_hbm.shape[1] :] = jnp.zeros((total_rows, 2 * c0), BF16)
     w1p_ref[0:c0, :] = jnp.zeros((c0, c1), BF16)
@@ -306,10 +315,13 @@
         return first_parts(x_ref, c * n, n, bias, w1p_ref, xs[c % 2], carry_ref)
 
     loads[0].wait()
+    for load in loads[1:]:
+        load.start()
     for k in range(PARTS):
         parts_of(0)(k)
     for w in weights:
         w.wait()
+    proj_load.start()
 
     def tap(k):
         if k == 3:

time: 44.2 us -> 43.7 us (0.989)
  Pallas kernels: 42.5 us -> 41.9 us
    pallas_call x1, Pallas kernels: 42.5 us -> 41.9 us  [shards(): pl.pallas_call(functools.partial(body, ring), out_shape=jax.ShapeDtypeStr...]
where the time goes in v5:
time: 43.7 us; the launch traced here: 43.6 us
  Pallas kernels  41.9 us (96%)
  other arithmetic  1.03 us (2%)
  between operations  0.67 us (2%)
    pallas_call x1, Pallas kernels, shards(): pl.pallas_call(functools.partial(body, ring), out_shape=jax.ShapeDtypeStr...  41.9 us
    broadcast_in_dim x1, other arithmetic, shards(): return jnp.where(live[:, None], out, jnp.zeros_like(out))[None]  1.02 us

profile of v5, /device:TPU:1, one launch (start us, length us, event | category | flops | bytes accessed | tf_op | source)
XLA Modules:
  0.0 43.6 jit_solution(15514766252125638755)
XLA Ops:
  0.7 41.9 %stem_attention.1 = bf16[1536,128]{1,0:T(8,128)(2,1)S(1)} custom-call(s32[1]{0:T(128)} %copy.8.count_ref, bf16[192,8192]{1,0:T(8,128)(2,1)} %bitcast.10, bf16[448,256]{1,0:T(8,128)(2,1)} %bitcast.11, f32[1,256]{1,0:T(1,128)} %bitcast.13, bf16[7,256,1024]{2,1,0:T(8,128)(2,1)} %w2_hbm.1, f32[1,1024]{1,0:T(1,128)} %bitcast.12, bf16[3,1024,1024]{2,1,0:T(8,128)(2,1)} %bitcast.9), custom_call_target="tpu_custom_call" | custom-call | tf_op jit(solution)/shard_map/stem_attention/pallas_call | solution.py:378
  42.6 1.0 %select_bitcast_fusion = bf16[1,1536,128]{2,1,0:T(8,128)(2,1)} fusion(bf16[1536,128]{1,0:T(8,128)(2,1)S(1)} %stem_attention.1, pred[1536]{0:T(1024)(128)(4,1)S(1)} %iota_compare_fusion), kind=kLoop, calls=%fused_computation | loop fusion | flops 196608 | bytes 787968 | tf_op jit(solution)/shard_map/broadcast_in_dim | solution.py:425
  (1 shorter events, 0.0 us)

commit v6 on v5

--- a/solution.py
+++ b/solution.py
@@ -279,14 +279,15 @@
 
     part_b = n
     part_a = total_rows - n
-    groups = [(0, send_a, got_a, part_a, 0), (1, send_b, got_b, part_b, part_a)]
+    groups = [(c, send_a, got_a, part_a, c * n) for c in range(CHUNKS - 1)]
+    groups.append((CHUNKS - 1, send_b, got_b, part_b, 0))
 
     def sends(group):
-        g, src, dst, part, _ = group
+        g, src, dst, part, off = group
         return [
             pltpu.make_async_remote_copy(
-                src_ref=src.at[lax.rem(me + i, ring)],
-                dst_ref=dst.at[:, pl.ds(pl.multiple_of(me * part, part), part)],
+                src_ref=src.at[lax.rem(me + i, ring), :, pl.ds(off, n)],
+                dst_ref=dst.at[:, pl.ds(pl.multiple_of(me * part + off, n), n)],
                 send_sem=send_sem.at[g, i - 1],
                 recv_sem=recv_sem.at[g, i - 1],
                 device_id=(rec, lax.rem(me + i, ring)),
@@ -296,18 +297,18 @@
         ]
 
     def project(group):
-        g, src, dst, part, start = group
+        g, src, dst, part, off = group
         width = dst.shape[2]
         for j in range(3):
-            mixed = dot(emb_ref[start : start + part, :], proj_ref[j])
+            mixed = dot(emb_ref[g * n : (g + 1) * n, :], proj_ref[j])
             if j == 0:
                 mixed = mixed * (LOG2E * HD**-0.5)
             mixed = mixed.astype(BF16)
             for peer in range(ring):
-                src[peer, j] = mixed[:, peer * width : (peer + 1) * width]
+                src[peer, j, off : off + n, :] = mixed[:, peer * width : (peer + 1) * width]
         for copy in sends(group):
             copy.start()
-        dst[:, pl.ds(pl.multiple_of(me * part, part), part), :] = src[me]
+        dst[:, pl.ds(pl.multiple_of(me * part + off, n), n), :] = src[me, :, off : off + n, :]
 
     xs = (xs_even, xs_odd)
 
@@ -341,16 +342,16 @@
         else:
             weave = lambda k: None
         second_layer(n, b2_ref, wt_ref, xs[c % 2], part_ref, emb_ref, c * n, weave)
-        if c == CHUNKS - 2:
+        if c == 0:
             proj_load.wait()
             pl.semaphore_wait(barrier, ring - 1)
-            project(groups[0])
-    project(groups[1])
-    for copy in sends(groups[0]):
-        copy.wait()
+        project(groups[c])
+    for group in groups[:-1]:
+        for copy in sends(group):
+            copy.wait()
 
     def between():
-        for copy in sends(groups[1]):
+        for copy in sends(groups[-1]):
             copy.wait()
 
     attend_parts(
@@ -404,8 +405,8 @@
             pltpu.SemaphoreType.DMA((3,)),
             pltpu.SemaphoreType.DMA((taps,)),
             pltpu.SemaphoreType.DMA,
-            pltpu.SemaphoreType.DMA((2, ring - 1)),
-            pltpu.SemaphoreType.DMA((2, ring - 1)),
+            pltpu.SemaphoreType.DMA((CHUNKS, ring - 1)),
+            pltpu.SemaphoreType.DMA((CHUNKS, ring - 1)),
         ],
         compiler_params=pltpu.CompilerParams(
             vmem_limit_bytes=52 * 1024 * 1024, collective_id=0, has_side_effects=True

time: 43.7 us -> 44 us (level)
  no operation moved by 1% of the time
where the time goes in v6:
time: 44 us; the launch traced here: 43.9 us
  Pallas kernels  42.2 us (96%)
  other arithmetic  1.03 us (2%)
  between operations  0.67 us (2%)
    pallas_call x1, Pallas kernels, shards(): pl.pallas_call(functools.partial(body, ring), out_shape=jax.ShapeDtypeStr...  42.2 us
    broadcast_in_dim x1, other arithmetic, shards(): return jnp.where(live[:, None], out, jnp.zeros_like(out))[None]  1.02 us

profile of v6, /device:TPU:1, one launch (start us, length us, event | category | flops | bytes accessed | tf_op | source)
XLA Modules:
  0.0 43.9 jit_solution(11394629506344738397)
XLA Ops:
  0.7 42.2 %stem_attention.1 = bf16[1536,128]{1,0:T(8,128)(2,1)S(1)} custom-call(s32[1]{0:T(128)} %copy.8.count_ref, bf16[192,8192]{1,0:T(8,128)(2,1)} %bitcast.10, bf16[448,256]{1,0:T(8,128)(2,1)} %bitcast.11, f32[1,256]{1,0:T(1,128)} %bitcast.13, bf16[7,256,1024]{2,1,0:T(8,128)(2,1)} %w2_hbm.1, f32[1,1024]{1,0:T(1,128)} %bitcast.12, bf16[3,1024,1024]{2,1,0:T(8,128)(2,1)} %bitcast.9), custom_call_target="tpu_custom_call" | custom-call | tf_op jit(solution)/shard_map/stem_attention/pallas_call | solution.py:379
  42.9 1.0 %select_bitcast_fusion = bf16[1,1536,128]{2,1,0:T(8,128)(2,1)} fusion(bf16[1536,128]{1,0:T(8,128)(2,1)S(1)} %stem_attention.1, pred[1536]{0:T(1024)(128)(4,1)S(1)} %iota_compare_fusion), kind=kLoop, calls=%fused_computation | loop fusion | flops 196608 | bytes 787968 | tf_op jit(solution)/shard_map/broadcast_in_dim | solution.py:426
  (1 shorter events, 0.0 us)
